TPU v7x, 128 devices: a whole 4x4x4 slice. The times are simulated.
128 devices in a mesh: face: 8 (over y, core), tile: 16 (over z, x).
Axes of the slice: x: 4, y: 4, z: 4, core: 2. Of those that a mesh axis runs over, the one named last changes fastest.
Arguments:
- met_src: bfloat16 [8192, 48, 128], P(('face', 'tile')), may hold values from -6 to 6
- intersection_weights: bfloat16 [8192, 128, 128], P(('face', 'tile')), may hold values from -0.5 to 0.5
- block_dest: int32 [8192], P(('face', 'tile')), may hold values from 0 to 127, as said below
- block_row: int32 [8192], P(('face', 'tile')), may hold values from 0 to 15
- tracers: float32 [250, 4, 128, 2048], P(None, None, 'face', 'tile'), may hold values from 0.1 to 10
- rate_coef: float32 [250, 12], replicated, may hold values from -1.75 to 1.75
- photo_coef: float32 [250], replicated, may hold values from 0.1 to 3
Outputs:
- met_tile: float32 [12, 4, 128, 2048], P(None, None, 'face', 'tile')
- species_out: float32 [250, 4, 128, 2048], P(None, None, 'face', 'tile')
Inputs may be any that keep to these rules, and one draw needn't show every extreme that they name: `block_dest`: each source owner (the 64 blocks of one device) names any one tile owner at most 2 times; in every draw some tile owner is named exactly 2 times by every source owner.
All inputs are finite; a program needn't handle non-finite values.
Results may differ from a plain program's by a relative error of at most 0.0029.
Values may be sent and summed in bfloat16 or wider, within the bound.
A program may use at most 128 MiB of HBM per device.

v0:
```python
import jax
import jax.numpy as jnp
from jax import lax
from jax.sharding import PartitionSpec as P

CAP = 2
ADV_STEPS = 2


def from_behind(shard, axis, by):
    devices = lax.axis_size(axis)
    return lax.ppermute(shard, axis, [(i, (i + by) % devices) for i in range(devices)])


def with_halo(block, sides, width):
    for axis, dim in sides:
        count = lax.axis_size(axis)
        forward = [(i, i + 1) for i in range(count - 1)]
        forward.append((count - 1, 0))
        backward = [(target, source) for source, target in forward]
        low = lax.ppermute(
            lax.slice_in_dim(block, block.shape[dim] - width, None, axis=dim), axis, forward
        )
        high = lax.ppermute(lax.slice_in_dim(block, 0, width, axis=dim), axis, backward)
        block = jnp.concatenate([low, block, high], axis=dim)
    return block


def deliver(packed, slot_label):
    arrived, labels = (
        lax.all_to_all(packed, ("face", "tile"), split_axis=0, concat_axis=0, tiled=True),
        lax.all_to_all(slot_label, ("face", "tile"), split_axis=0, concat_axis=0, tiled=True),
    )
    return (arrived, labels)


def local(met_src, intersection_weights, block_dest, block_row, tracers, rate_coef, photo_coef):
    n_face = lax.axis_size("face")
    n_tile = lax.axis_size("tile")
    owner_count = n_face * n_tile
    blocks, levfields, cell_count = met_src.shape
    nfields = rate_coef.shape[1]
    levels = levfields // nfields
    rows_x = tracers.shape[2]
    slot_count = owner_count * CAP
    owners = jnp.arange(owner_count, dtype=jnp.int32)
    matches = (block_dest[:, None] == owners[None, :]).astype(jnp.int32)
    earlier_count = jnp.cumsum(matches, axis=0) - 1
    own_rank = jnp.sum(earlier_count * matches, axis=1)
    position = block_dest * CAP + own_rank
    placer = (jnp.arange(slot_count, dtype=jnp.int32)[:, None] == position[None, :]).astype(
        jnp.bfloat16
    )
    slot_label = (
        jnp.dot(placer, (block_row + 1).astype(jnp.bfloat16), preferred_element_type=jnp.float32)
        - 1.0
    ).astype(jnp.bfloat16)
    contrib = jnp.einsum(
        "sfi,sij->sfj", met_src, intersection_weights, preferred_element_type=jnp.float32
    ).astype(jnp.bfloat16)
    payload = contrib.reshape(blocks, levfields * cell_count)
    packed = jnp.dot(placer, payload, preferred_element_type=jnp.float32).astype(jnp.bfloat16)
    arrived, labels = deliver(packed, slot_label)
    received = arrived.reshape(slot_count, levfields, cell_count)
    row_values = jnp.arange(rows_x).astype(jnp.bfloat16)
    chooser = (labels[:, None] == row_values[None, :]).astype(jnp.bfloat16)
    met_flat = jnp.einsum("rt,rfc->ftc", chooser, received, preferred_element_type=jnp.float32)
    met_tile = met_flat.reshape(nfields, levels, rows_x, cell_count)
    courant_x = 0.3 * jnp.tanh(met_tile[0])
    courant_y = 0.3 * jnp.tanh(met_tile[1])
    west_row = from_behind(courant_x[:, -1:, :], "face", 1)
    south_column = from_behind(courant_y[:, :, -1:], "tile", 1)
    courant_xe = jnp.concatenate([west_row, courant_x], axis=1)
    courant_ye = jnp.concatenate([south_column, courant_y], axis=2)
    amount = tracers
    for substep in range(ADV_STEPS):
        padded = with_halo(amount, (("face", 2), ("tile", 3)), 1)
        lower_x = padded[:, :, 0 : rows_x + 1, 1:-1]
        upper_x = padded[:, :, 1 : rows_x + 2, 1:-1]
        flux_x = jnp.maximum(courant_xe, 0.0) * lower_x + jnp.minimum(courant_xe, 0.0) * upper_x
        lower_y = padded[:, :, 1:-1, 0 : cell_count + 1]
        upper_y = padded[:, :, 1:-1, 1 : cell_count + 2]
        flux_y = jnp.maximum(courant_ye, 0.0) * lower_y + jnp.minimum(courant_ye, 0.0) * upper_y
        amount = (
            padded[:, :, 1:-1, 1:-1]
            - (flux_x[:, :, 1:, :] - flux_x[:, :, :-1, :])
            - (flux_y[:, :, :, 1:] - flux_y[:, :, :, :-1])
        )
    column_depth = jnp.cumsum(jax.nn.softplus(met_tile[2]), axis=0)
    light = jnp.exp(-column_depth)
    exponent = (
        jnp.einsum("sf,flxy->slxy", rate_coef, met_tile, precision=lax.Precision.HIGHEST)
        + photo_coef[:, None, None, None] * light[None]
    )
    species_out = amount / (1.0 + jax.nn.softplus(exponent))
    return (met_tile, species_out)


def solution(mesh):
    return jax.shard_map(
        local,
        mesh=mesh,
        in_specs=(
            P(("face", "tile"), None, None),
            P(("face", "tile"), None, None),
            P(("face", "tile")),
            P(("face", "tile")),
            P(None, None, "face", "tile"),
            P(),
            P(),
        ),
        out_specs=(P(None, None, "face", "tile"), P(None, None, "face", "tile")),
        check_vma=False,
    )
```

profile of v0, /device:TPU:0, one launch (start us, length us, event | category | flops | bytes accessed | tf_op | source)
XLA Modules:
  0.0 202.9 jit_solution(7858804888711089524)
XLA Ops:
  0.6 0.9 fusion.36
  1.6 0.8 select_reduce_fusion
  3.1 0.8 fusion.20
  3.9 0.8 all_to_all.16
  4.7 11.2 %all-to-all-start.1 = ((bf16[128,2,1]{1,2,0:T(2,128)(2,1)}), bf16[128,2,1]{1,2,0:T(2,128)(2,1)S(1)}, u32[]{:S(2)}, u32[]{:S(2)}) async-start(bf16[128,2,1]{1,2,0:T(2,128)(2,1)} %all_to_all.16), calls=%async_computation.1 | async-start | bytes 131072 | tf_op jit(solution)/shard_map/all_to_all | solution.py:32
  15.9 1.8 convolution_convert_fusion.1
  17.8 2.6 %convolution_convert_fusion = bf16[256,6144]{1,0:T(8,128)(2,1)} fusion(bf16[8,8,48,128]{3,2,1,0:T(8,128)(2,1)S(1)} %bitcast.27, s32[64]{0:T(128)S(1)} %multiply_add_fusion), kind=kOutput, calls=%fused_computation.36 | convolution fusion | flops 202915840 | bytes 3932416 | tf_op jit(solution)/shard_map/dot_general | solution.py:62
  20.4 7.0 %all_to_all.12 = bf16[128,2,6144]{2,1,0:T(2,128)(2,1)} reshape(bf16[256,6144]{1,0:T(8,128)(2,1)} %convolution_convert_fusion) | data formatting | bytes 6291456 | tf_op jit(solution)/shard_map/all_to_all | solution.py:31
  27.4 10.2 %all-to-all-start = ((bf16[128,2,6144]{2,1,0:T(2,128)(2,1)}), bf16[128,2,6144]{2,1,0:T(2,128)(2,1)}, u32[]{:S(2)}, u32[]{:S(2)}) async-start(bf16[128,2,6144]{2,1,0:T(2,128)(2,1)} %all_to_all.12), calls=%async_computation | async-start | bytes 6291456 | tf_op jit(solution)/shard_map/all_to_all | solution.py:31
  37.7 10.0 %copy.32 = f32[250,4,16,128]{0,3,2,1:T(8,128)} copy(f32[250,4,16,128]{3,2,1,0:T(8,128)} %param.11) | data formatting | bytes 16384000 | tf_op args[4]
  47.7 1.3 fusion.50
  48.9 1.9 collective-permute-start.2
  51.2 24.6 %collective-permute-done.2 = f32[250,4,1,128]{0,3,2,1:T(8,128)S(1)} collective-permute-done((f32[250,4,1,128]{0,3,2,1:T(8,128)S(1)}, f32[250,4,1,128]{0,3,2,1:T(8,128)S(1)}, u32[]{:S(2)}, u32[]{:S(2)}) %collective-permute-start.2) | collective-permute-done | bytes 512032 | tf_op jit(solution)/shard_map/ppermute | solution.py:24
  75.8 3.3 %collective-permute-done.1 = f32[250,4,1,128]{0,3,2,1:T(8,128)S(1)} collective-permute-done((f32[250,4,1,128]{0,3,2,1:T(8,128)S(1)}, f32[250,4,1,128]{0,3,2,1:T(8,128)S(1)}, u32[]{:S(2)}, u32[]{:S(2)}) %collective-permute-start.1) | collective-permute-done | bytes 512032 | tf_op jit(solution)/shard_map/ppermute | solution.py:21
  79.1 1.3 pad_maximum_fusion.17
  80.4 5.8 %collective-permute-start.5 = (f32[250,4,18,1]{0,3,2,1:T(1,128)S(1)}, f32[250,4,18,1]{0,3,2,1:T(1,128)S(1)}, u32[]{:S(2)}, u32[]{:S(2)}) collective-permute-start(f32[250,4,18,1]{0,3,2,1:T(1,128)S(1)} %get-tuple-element.11), channel_id=1, source_target_pairs={{1,0},{2,1},{3,2},{4,3},{5,4},{6,5},{7,6},{8,7},{9,8},{10,9},{11,1... | collective-permute-start | bytes 216008 | tf_op jit(solution)/shard_map/ppermute | solution.py:24
  86.2 8.0 %reshape.102 = bf16[256,48,128]{2,1,0:T(8,128)(2,1)} reshape(bf16[128,2,6144]{2,1,0:T(2,128)(2,1)} %all-to-all-done) | data formatting | bytes 6291456 | tf_op jit(solution)/shard_map/reshape | solution.py:64
  94.2 2.6 %fusion.14 = f32[48,128,16]{1,2,0:T(8,128)S(1)} fusion(bf16[256,48,128]{2,1,0:T(8,128)(2,1)} %reshape.102, bf16[256]{0:T(256)(128)(2,1)S(1)} %eq.47, bf16[16]{0:T(256)(128)(2,1)S(1)} %iota_convert_fusion), kind=kOutput, calls=%fused_computation.37 | convolution fusion | flops 50335744 | bytes 3539488 | tf_op jit(solution)/shard_map/rt,rfc->ftc/dot_general | solution.py:67
  97.0 7.1 %collective-permute-done.3 = f32[4,16,1]{2,1,0:T(8,128)S(1)} collective-permute-done((f32[4,16,1]{2,1,0:T(8,128)S(1)}, f32[4,16,1]{2,1,0:T(8,128)S(1)}, u32[]{:S(2)}, u32[]{:S(2)}) %collective-permute-start.3) | collective-permute-done | bytes 288 | tf_op jit(solution)/shard_map/ppermute | solution.py:12
  104.9 11.6 %fusion.4 = f32[250,4,16,129]{0,3,2,1:T(8,128)} fusion(f32[250,4,18,1]{0,3,2,1:T(1,128)S(1)} %collective-permute-done.5, f32[250,4,1,128]{0,3,2,1:T(8,128)S(1)} %collective-permute-done.2, f32[250,4,16,128]{0,3,2,1:T(8,128)} %copy.32, f32[250,4,1,128]{0,3,2,1:T(8,128)S(1)} %collective-permute-done.1, f32[250,4,18,1]{0,3,2,1:T(1,128)S(1)} %collective-permute-done.4, ...), kind=kLoop, calls=%fused_computation.12 | loop fusion | flops 18576000 | bytes 17682048 | tf_op jit(solution)/shard_map/add | solution.py:83
  116.6 6.0 %fusion.6 = f32[250,4,17,128]{0,3,2,1:T(8,128)} fusion(f32[250,4,16,128]{0,3,2,1:T(8,128)S(1)} %bitcast.26, f32[250,4,1,128]{0,3,2,1:T(8,128)S(1)} %collective-permute-done.1, f32[250,4,1,128]{0,3,2,1:T(8,128)S(1)} %collective-permute-done.2, f32[4,17,128]{2,1,0:T(8,128)S(1)} %get-tuple-element.21, f32[4,17,128]{2,1,0:T(8,128)S(1)} %get-tuple-element.20), kind=kLoop, calls=%fused_computation.20 | loop fusion | flops 10880000 | bytes 17989632 | tf_op jit(solution)/shard_map/add | solution.py:80
  122.6 19.2 %fusion.12 = f32[250,4,16,128]{0,3,2,1:T(8,128)} fusion(f32[250,4,16,129]{0,3,2,1:T(8,128)} %fusion.4, f32[250,4,16,128]{0,3,2,1:T(8,128)} %copy.32, f32[250,4,17,128]{0,3,2,1:T(8,128)} %fusion.6), kind=kLoop, calls=%fused_computation.32 | loop fusion | flops 8192000 | bytes 49152000 | tf_op jit(solution)/shard_map/sub | solution.py:85
  141.8 1.4 fusion.49
  143.7 6.2 %collective-permute-done.7 = f32[250,4,1,128]{0,3,2,1:T(8,128)S(1)} collective-permute-done((f32[250,4,1,128]{0,3,2,1:T(8,128)S(1)}, f32[250,4,1,128]{0,3,2,1:T(8,128)S(1)}, u32[]{:S(2)}, u32[]{:S(2)}) %collective-permute-start.7) | collective-permute-done | bytes 512032 | tf_op jit(solution)/shard_map/ppermute | solution.py:24
  149.9 3.1 %collective-permute-done.6 = f32[250,4,1,128]{0,3,2,1:T(8,128)S(1)} collective-permute-done((f32[250,4,1,128]{0,3,2,1:T(8,128)S(1)}, f32[250,4,1,128]{0,3,2,1:T(8,128)S(1)}, u32[]{:S(2)}, u32[]{:S(2)}) %collective-permute-start.6) | collective-permute-done | bytes 512032 | tf_op jit(solution)/shard_map/ppermute | solution.py:21
  153.0 1.3 pad_maximum_fusion.14
  154.4 1.9 collective-permute-start.9
  156.6 6.0 %fusion.7 = f32[250,4,17,128]{0,3,2,1:T(8,128)} fusion(f32[250,4,16,128]{0,3,2,1:T(8,128)S(1)} %copy-done.2, f32[250,4,1,128]{0,3,2,1:T(8,128)S(1)} %collective-permute-done.6, f32[250,4,1,128]{0,3,2,1:T(8,128)S(1)} %collective-permute-done.7, f32[4,17,128]{2,1,0:T(8,128)S(1)} %get-tuple-element.21, f32[4,17,128]{2,1,0:T(8,128)S(1)} %get-tuple-element.20), kind=kLoop, calls=%fused_computation.23 | loop fusion | flops 10880000 | bytes 17989632 | tf_op jit(solution)/shard_map/add | solution.py:80
  162.6 1.4 collective-permute-done.8
  164.0 6.8 %fusion.1 = f32[250,4,16,129]{0,3,2,1:T(8,128)} fusion(f32[250,4,18,1]{0,3,2,1:T(1,128)S(1)} %collective-permute-done.9, f32[250,4,1,128]{0,3,2,1:T(8,128)S(1)} %collective-permute-done.7, f32[250,4,16,128]{0,3,2,1:T(8,128)S(1)} %copy-done.2, f32[250,4,1,128]{0,3,2,1:T(8,128)S(1)} %collective-permute-done.6, f32[250,4,18,1]{0,3,2,1:T(1,128)S(1)} %collective-permute-done.8, ...), kind=kLoop, calls=%fused_computation.3 | loop fusion | flops 18576000 | bytes 17682048 | tf_op jit(solution)/shard_map/add | solution.py:83
  170.8 22.1 %fusion.9 = f32[250,4,16,128]{0,3,2,1:T(8,128)} fusion(f32[250,4,16,129]{0,3,2,1:T(8,128)} %fusion.1, f32[250,4,16,128]{0,3,2,1:T(8,128)} %fusion.12, f32[250,4,17,128]{0,3,2,1:T(8,128)} %fusion.7, f32[4,16,128]{2,1,0:T(8,128)S(1)} %fusion.16, f32[250]{0:T(256)S(1)} %copy-done.5, f32[12,4,16,128]{3,2,1,0:T(8,128)S(1)} %bitcast.30, f32[250,12]{0,1:T(8,128)S(1)} %copy-done.4), kind=kOutput, calls=%fused_computation.26 | convolution fusion | flops 323584000 | bytes 49590984 | tf_op jit(solution)/shard_map/sf,flxy->slxy/dot_general | solution.py:92
  192.9 10.0 %copy.35 = f32[250,4,16,128]{3,2,1,0:T(8,128)} copy(f32[250,4,16,128]{0,3,2,1:T(8,128)} %fusion.9) | data formatting | bytes 16384000
  (42 shorter events, 3.1 us)
Async XLA Ops:
  0.6 15.3 %copy-start = (bf16[64,128,128]{2,1,0:T(8,128)(2,1)S(1)}, bf16[64,128,128]{2,1,0:T(8,128)(2,1)}, u32[]{:S(2)}) copy-start(bf16[64,128,128]{2,1,0:T(8,128)(2,1)} %param.8) | copy-start | bytes 6291460
  4.7 22.7 %all-to-all-start.1 = ((bf16[128,2,1]{1,2,0:T(2,128)(2,1)}), bf16[128,2,1]{1,2,0:T(2,128)(2,1)S(1)}, u32[]{:S(2)}, u32[]{:S(2)}) async-start(bf16[128,2,1]{1,2,0:T(2,128)(2,1)} %all_to_all.16), calls=%async_computation.1 | async-start | bytes 131072 | tf_op jit(solution)/shard_map/all_to_all | solution.py:32
  27.4 58.8 %all-to-all-start = ((bf16[128,2,6144]{2,1,0:T(2,128)(2,1)}), bf16[128,2,6144]{2,1,0:T(2,128)(2,1)}, u32[]{:S(2)}, u32[]{:S(2)}) async-start(bf16[128,2,6144]{2,1,0:T(2,128)(2,1)} %all_to_all.12), calls=%async_computation | async-start | bytes 6291456 | tf_op jit(solution)/shard_map/all_to_all | solution.py:31
  48.9 26.8 %collective-permute-start.2 = (f32[250,4,1,128]{0,3,2,1:T(8,128)S(1)}, f32[250,4,1,128]{0,3,2,1:T(8,128)S(1)}, u32[]{:S(2)}, u32[]{:S(2)}) collective-permute-start(f32[250,4,1,128]{0,3,2,1:T(8,128)S(1)} %get-tuple-element.15), channel_id=1, source_target_pairs={{16,0},{32,16},{48,32},{64,48},{80,64},{96,80},{112,96},{0,112},{1... | collective-permute-start | bytes 1536008 | tf_op jit(solution)/shard_map/ppermute | solution.py:24
  50.8 28.2 %collective-permute-start.1 = (f32[250,4,1,128]{0,3,2,1:T(8,128)S(1)}, f32[250,4,1,128]{0,3,2,1:T(8,128)S(1)}, u32[]{:S(2)}, u32[]{:S(2)}) collective-permute-start(f32[250,4,1,128]{0,3,2,1:T(8,128)S(1)} %get-tuple-element.14), channel_id=1, source_target_pairs={{0,16},{16,32},{32,48},{48,64},{64,80},{80,96},{96,112},{112,0},{1... | collective-permute-start | bytes 1536008 | tf_op jit(solution)/shard_map/ppermute | solution.py:21
  80.4 23.8 %collective-permute-start.5 = (f32[250,4,18,1]{0,3,2,1:T(1,128)S(1)}, f32[250,4,18,1]{0,3,2,1:T(1,128)S(1)}, u32[]{:S(2)}, u32[]{:S(2)}) collective-permute-start(f32[250,4,18,1]{0,3,2,1:T(1,128)S(1)} %get-tuple-element.11), channel_id=1, source_target_pairs={{1,0},{2,1},{3,2},{4,3},{5,4},{6,5},{7,6},{8,7},{9,8},{10,9},{11,1... | collective-permute-start | bytes 216008 | tf_op jit(solution)/shard_map/ppermute | solution.py:24
  94.2 22.4 %slice-start = ((s8[8388608]{0:T(1024)(128)(4,1)}), s8[4194304]{0:T(1024)(128)(4,1)S(1)}, s32[]{:S(2)}) async-start(s8[8388608]{0:T(1024)(128)(4,1)} %bitcast.25), calls=%async_computation.2 | async-start | bytes 8388608
  96.8 74.0 %copy-start.3 = (f32[48,128,16]{1,2,0:T(8,128)}, f32[48,128,16]{1,2,0:T(8,128)S(1)}, u32[]{:S(2)}) copy-start(f32[48,128,16]{1,2,0:T(8,128)S(1)} %fusion.14) | copy-start | bytes 1179652
  96.9 7.2 %collective-permute-start.3 = (f32[4,16,1]{2,1,0:T(8,128)S(1)}, f32[4,16,1]{2,1,0:T(8,128)S(1)}, u32[]{:S(2)}, u32[]{:S(2)}) collective-permute-start(f32[4,16,1]{2,1,0:T(8,128)S(1)} %slice.122), channel_id=1, source_target_pairs={{0,1},{1,2},{2,3},{3,4},{4,5},{5,6},{6,7},{7,8},{8,9},{9,10},{10,1... | collective-permute-start | bytes 776 | tf_op jit(solution)/shard_map/ppermute | solution.py:12
  96.9 8.0 %collective-permute-start.4 = (f32[250,4,18,1]{0,3,2,1:T(1,128)S(1)}, f32[250,4,18,1]{0,3,2,1:T(1,128)S(1)}, u32[]{:S(2)}, u32[]{:S(2)}) collective-permute-start(f32[250,4,18,1]{0,3,2,1:T(1,128)S(1)} %get-tuple-element.10), channel_id=1, source_target_pairs={{0,1},{1,2},{2,3},{3,4},{4,5},{5,6},{6,7},{7,8},{8,9},{9,10},{10,1... | collective-permute-start | bytes 216008 | tf_op jit(solution)/shard_map/ppermute | solution.py:21
  97.0 19.5 %collective-permute-start = (f32[4,1,128]{2,1,0:T(1,128)S(1)}, f32[4,1,128]{2,1,0:T(1,128)S(1)}, u32[]{:S(2)}, u32[]{:S(2)}) collective-permute-start(f32[4,1,128]{2,1,0:T(1,128)S(1)} %slice.116), channel_id=1, source_target_pairs={{0,16},{16,32},{32,48},{48,64},{64,80},{80,96},{96,112},{112,0},{1... | collective-permute-start | bytes 6152 | tf_op jit(solution)/shard_map/ppermute | solution.py:12
  104.9 11.7 %slice-start.1 = ((s8[8388608]{0:T(1024)(128)(4,1)}), s8[4194304]{0:T(1024)(128)(4,1)S(1)}, s32[]{:S(2)}) async-start(s8[8388608]{0:T(1024)(128)(4,1)} %bitcast.25), calls=%async_computation.3 | async-start | bytes 8388608
  141.8 14.9 %copy-start.2 = (f32[250,4,16,128]{0,3,2,1:T(8,128)S(1)}, f32[250,4,16,128]{0,3,2,1:T(8,128)}, u32[]{:S(2)}) copy-start(f32[250,4,16,128]{0,3,2,1:T(8,128)} %fusion.12) | copy-start | bytes 24576004
  143.2 6.7 %collective-permute-start.7 = (f32[250,4,1,128]{0,3,2,1:T(8,128)S(1)}, f32[250,4,1,128]{0,3,2,1:T(8,128)S(1)}, u32[]{:S(2)}, u32[]{:S(2)}) collective-permute-start(f32[250,4,1,128]{0,3,2,1:T(8,128)S(1)} %get-tuple-element.13), channel_id=1, source_target_pairs={{16,0},{32,16},{48,32},{64,48},{80,64},{96,80},{112,96},{0,112},{1... | collective-permute-start | bytes 1536008 | tf_op jit(solution)/shard_map/ppermute | solution.py:24
  143.2 9.8 %collective-permute-start.6 = (f32[250,4,1,128]{0,3,2,1:T(8,128)S(1)}, f32[250,4,1,128]{0,3,2,1:T(8,128)S(1)}, u32[]{:S(2)}, u32[]{:S(2)}) collective-permute-start(f32[250,4,1,128]{0,3,2,1:T(8,128)S(1)} %get-tuple-element.12), channel_id=1, source_target_pairs={{0,16},{16,32},{32,48},{48,64},{64,80},{80,96},{96,112},{112,0},{1... | collective-permute-start | bytes 1536008 | tf_op jit(solution)/shard_map/ppermute | solution.py:21
  154.4 8.2 %collective-permute-start.9 = (f32[250,4,18,1]{0,3,2,1:T(1,128)S(1)}, f32[250,4,18,1]{0,3,2,1:T(1,128)S(1)}, u32[]{:S(2)}, u32[]{:S(2)}) collective-permute-start(f32[250,4,18,1]{0,3,2,1:T(1,128)S(1)} %get-tuple-element.9), channel_id=1, source_target_pairs={{1,0},{2,1},{3,2},{4,3},{5,4},{6,5},{7,6},{8,7},{9,8},{10,9},{11,1... | collective-permute-start | bytes 216008 | tf_op jit(solution)/shard_map/ppermute | solution.py:24
  156.3 7.7 %collective-permute-start.8 = (f32[250,4,18,1]{0,3,2,1:T(1,128)S(1)}, f32[250,4,18,1]{0,3,2,1:T(1,128)S(1)}, u32[]{:S(2)}, u32[]{:S(2)}) collective-permute-start(f32[250,4,18,1]{0,3,2,1:T(1,128)S(1)} %get-tuple-element.8), channel_id=1, source_target_pairs={{0,1},{1,2},{2,3},{3,4},{4,5},{5,6},{6,7},{7,8},{8,9},{9,10},{10,1... | collective-permute-start | bytes 216008 | tf_op jit(solution)/shard_map/ppermute | solution.py:21
  162.6 8.2 %copy-start.4 = (f32[250,12]{0,1:T(8,128)S(1)}, f32[250,12]{0,1:T(8,128)}, u32[]{:S(2)}) copy-start(f32[250,12]{0,1:T(8,128)} %param.12) | copy-start | bytes 36004
  162.6 8.2 %copy-start.5 = (f32[250]{0:T(256)S(1)}, f32[250]{0:T(256)}, u32[]{:S(2)}) copy-start(f32[250]{0:T(256)} %param.13) | copy-start | bytes 3004
  170.8 32.2 %copy-start.1 = (bf16[64,128,128]{2,1,0:T(8,128)(2,1)S(1)}, bf16[64,128,128]{2,1,0:T(8,128)(2,1)}, u32[]{:S(2)}) copy-start(bf16[64,128,128]{2,1,0:T(8,128)(2,1)} %param.8) | copy-start | bytes 6291460
where the time goes:
time: 204 us; the launch traced here: 203 us
  other arithmetic  55 us (27%)
  waiting for transfers between devices  46.4 us (23%)
  local copies, waits for them, and re-layouts  38.8 us (19%)
  starting transfers between devices  32 us (16%)
  matrix products  30 us (15%)
    ppermute x4, waiting for transfers between devices, with_halo(): lax.ppermute(lax.slice_in_dim(block, 0, width, axis=dim), axis, backward)  30.8 us
    dot_general x1, matrix products, local(): jnp.einsum('sf,flxy->slxy', rate_coef, met_tile, precision=lax.Precision....  22.1 us
    unnamed x18, local copies, waits for them, and re-layouts  20 us
    sub x1, other arithmetic, local(): padded[:, :, 1:-1, 1:-1] - (flux_x[:, :, 1:, :] - flux_x[:, :, :-1, :])  19.2 us
    add x2, other arithmetic, local(): jnp.maximum(courant_ye, 0.0) * lower_y  18.4 us
    add x2, other arithmetic, local(): jnp.maximum(courant_xe, 0.0) * lower_x  11.9 us
    all_to_all x1, starting transfers between devices, deliver(): lax.all_to_all(slot_label, ('face', 'tile'), split_axis=0, concat_axis=0,...  11.2 us
    all_to_all x1, starting transfers between devices, deliver(): lax.all_to_all(packed, ('face', 'tile'), split_axis=0, concat_axis=0, til...  10.2 us
  transfers between devices with their start and end apart: 12, of which 7 were waited for; matrix products, arithmetic and copies ran while one was open for 23% of the time, Pallas kernels for 0%

commit v1 on v0

--- a/solution.py
+++ b/solution.py
@@ -1,9 +1,241 @@
+import functools
 import jax
 import jax.numpy as jnp
 from jax import lax
+from jax.experimental import pallas as pl
+from jax.experimental.pallas import tpu as pltpu
 from jax.sharding import PartitionSpec as P
 
-CAP = 2
+MESH = pl.DeviceIdType.MESH
+F32 = jnp.float32
+BF16 = jnp.bfloat16
+PARTS = (("x", "y", "z"), ("y", "z", "x"), ("z", "x", "y"))
+RING = 4
+ITEMS = 64
+SLAB = 16 + 16 * ITEMS
+CUT = 16 + 8 * ITEMS
+PER_PART = 22
+
+
+def whereabouts():
+    face = lax.axis_index("face")
+    tile = lax.axis_index("tile")
+    return {"x": lax.rem(tile, 4), "y": face // 2, "z": tile // 4, "c": lax.rem(face, 2)}
+
+
+def device(at):
+    return (at["y"] * 2 + at["c"], at["z"] * 4 + at["x"])
+
+
+def moved(at, dim, by):
+    there = dict(at)
+    there[dim] = 1 - at[dim] if dim == "c" else lax.rem(at[dim] + by, RING)
+    return there
+
+
+class Copies:
+    def __init__(self, send, recv):
+        self.send, self.recv, self.made = send, recv, {}
+
+    def start(self, index, src, dst, there):
+        copy = pltpu.make_async_remote_copy(
+            src_ref=src,
+            dst_ref=dst,
+            send_sem=self.send.at[index],
+            recv_sem=self.recv.at[index],
+            device_id=device(there),
+            device_id_type=MESH,
+        )
+        copy.start()
+        self.made[index] = copy
+
+    def arrived(self, *indices):
+        for index in indices:
+            self.made[index].wait_recv()
+
+    def sent(self):
+        for copy in self.made.values():
+            copy.wait_send()
+
+
+def regrid(at, copies, met_ref, weight_ref, key_ref, mx_ref, cs, gath, mask, part_sum, relay, ring_in, full, cut_sum, last_in):
+    me = {p: at[dims[0]] * 2 + at["c"] for p, dims in enumerate(PARTS)}
+    low, high = pl.ds(0, CUT), pl.ds(CUT, SLAB - CUT)
+
+    for p, (first, second, third) in enumerate(PARTS):
+        base, own = p * PER_PART, gath.at[p, me[p]]
+        nxt, prv, mate = moved(at, first, 1), moved(at, first, 3), moved(at, "c", 1)
+        gath[p, me[p], 0:16, :] = key_ref[p]
+        gath[p, me[p], 16:SLAB, :] = cs[p * 1024 : (p + 1) * 1024, :].astype(BF16)
+        copies.start(base + 0, own.at[low], own.at[low], nxt)
+        copies.start(base + 2, own.at[high], own.at[high], prv)
+        copies.start(base + 1, own.at[high], own.at[high], nxt)
+        copies.start(base + 3, own.at[low], own.at[low], prv)
+        copies.start(base + 4, own, own, mate)
+
+    def pass_on(p, wait, half, step, index, there):
+        base = p * PER_PART
+        slot = lax.rem(at[PARTS[p][0]] + step, RING) * 2 + at["c"]
+        ref = gath.at[p, slot, half]
+        if wait is not None:
+            copies.arrived(base + wait)
+        copies.start(base + index, ref, ref, there)
+
+    for p, (first, second, third) in enumerate(PARTS):
+        pass_on(p, 0, low, 3, 5, moved(at, first, 1))
+        pass_on(p, None, low, 3, 6, moved(at, "c", 1))
+        pass_on(p, 2, high, 1, 7, moved(at, first, 3))
+        pass_on(p, None, high, 1, 8, moved(at, "c", 1))
+    for p, (first, second, third) in enumerate(PARTS):
+        pass_on(p, 1, high, 3, 9, moved(at, "c", 1))
+        pass_on(p, 3, low, 1, 10, moved(at, "c", 1))
+    for p, (first, second, third) in enumerate(PARTS):
+        pass_on(p, 5, low, 2, 11, moved(at, "c", 1))
+        pass_on(p, 7, high, 2, 12, moved(at, "c", 1))
+
+    lane = lax.broadcasted_iota(jnp.int32, (1, 128), 1)
+    rows = lax.broadcasted_iota(jnp.int32, (256, 128), 0).astype(F32)
+    h0, h1 = pl.ds(0, 512), pl.ds(512, 512)
+
+    for p, (first, second, third) in enumerate(PARTS):
+        base = p * PER_PART
+        copies.arrived(*[base + k for k in (4, 6, 8, 9, 10, 11, 12)])
+        mine = me[p].astype(F32)
+        for a in range(RING):
+            k0 = gath[p, 2 * a, 0:16, :].astype(F32)
+            k1 = gath[p, 2 * a + 1, 0:16, :].astype(F32)
+            high_key = jnp.where(lane < ITEMS, k0[0:1, :], k1[0:1, :])
+            low_key = jnp.where(lane < ITEMS, k0[8:9, :], k1[8:9, :])
+            key = jnp.where(high_key == mine, low_key, -1.0)
+            mask[:, a * 128 : (a + 1) * 128] = jnp.where(rows == key, 1.0, 0.0).astype(BF16)
+
+        @pl.loop(0, 8)
+        def _(pair):
+            def level(fl):
+                start = pl.multiple_of(16 + fl * ITEMS, 16)
+                return jnp.concatenate([gath[p, s, pl.ds(start, ITEMS), :] for s in range(8)], axis=0)
+
+            rhs = jnp.concatenate([level(2 * pair), level(2 * pair + 1)], axis=1)
+            out = jnp.dot(mask[...], rhs, preferred_element_type=F32).astype(BF16)
+            for side in range(2):
+                start = pl.multiple_of((2 * pair + side) * 64, 64)
+                for b in range(RING):
+                    part_sum[p, b, pl.ds(start, 64), :] = out[b * 64 : (b + 1) * 64, side * 128 : (side + 1) * 128]
+
+        nxt, prv = moved(at, second, 1), moved(at, second, 3)
+        up, down, far = nxt[second], prv[second], lax.rem(at[second] + 2, RING)
+        copies.start(base + 13, part_sum.at[p, far, h0], relay.at[p, 0], nxt)
+        copies.start(base + 14, part_sum.at[p, far, h1], relay.at[p, 1], prv)
+        copies.start(base + 15, part_sum.at[p, up, h1], ring_in.at[p, 0, h1], nxt)
+        copies.start(base + 16, part_sum.at[p, down, h0], ring_in.at[p, 1, h0], prv)
+
+    for p, (first, second, third) in enumerate(PARTS):
+        base = p * PER_PART
+        nxt, prv = moved(at, second, 1), moved(at, second, 3)
+        for index, side, there, half in ((13, 0, nxt, h0), (14, 1, prv, h1)):
+            copies.arrived(base + index)
+            to = there[second]
+            total = part_sum[p, to, half, :].astype(F32) + relay[p, side].astype(F32)
+            part_sum[p, to, half, :] = total.astype(BF16)
+            copies.start(base + index + 4, part_sum.at[p, to, half], ring_in.at[p, side, half], there)
+
+    for p, (first, second, third) in enumerate(PARTS):
+        base = p * PER_PART
+        copies.arrived(*[base + k for k in (15, 16, 17, 18)])
+        own = at[second]
+
+        @pl.loop(0, 16)
+        def _(fl):
+            start = pl.multiple_of(fl * 64, 64)
+            block = pl.ds(start, 64)
+            total = part_sum[p, own, block, :].astype(F32) + ring_in[p, 0, block, :].astype(F32) + ring_in[p, 1, block, :].astype(F32)
+            full[p, block, :] = total
+            narrow = total.astype(BF16)
+            for c in range(RING):
+                cut_sum[p, c, pl.ds(pl.multiple_of(fl * 16, 16), 16), :] = narrow[c * 16 : (c + 1) * 16, :]
+
+        for k, by in enumerate((1, 3, 2)):
+            there = moved(at, third, by)
+            copies.start(base + 19 + k, cut_sum.at[p, there[third]], last_in.at[p, k], there)
+
+    for p, (first, second, third) in enumerate(PARTS):
+        base = p * PER_PART
+        copies.arrived(base + 19, base + 20, base + 21)
+        for fl in range(16):
+            start = pl.multiple_of(fl * 64 + at[third] * 16, 16)
+            here = slice(fl * 16, fl * 16 + 16)
+            total = full[p, pl.ds(start, 16), :]
+            for k in range(3):
+                total = total + last_in[p, k, here, :].astype(F32)
+            mx_ref[p * 256 + fl * 16 : p * 256 + fl * 16 + 16, :] = total
+
+
+def contributions(met_ref, weight_ref, cs):
+    @pl.loop(0, ITEMS // 4)
+    def _(group):
+        for k in range(4):
+            s = group * 4 + k
+            cs[pl.ds(s, 48, stride=ITEMS), :] = jnp.dot(met_ref[s], weight_ref[s], preferred_element_type=F32)
+
+
+def greet(at):
+    barrier = pltpu.get_barrier_semaphore()
+    peers = [moved(at, dim, by) for dim in ("x", "y", "z") for by in (1, 2, 3)] + [moved(at, "c", 1)]
+    for there in peers:
+        pl.semaphore_signal(barrier, inc=1, device_id=device(there), device_id_type=MESH)
+    return barrier, len(peers)
+
+
+REGRID_SCRATCH = [
+    pltpu.VMEM((48 * ITEMS, 128), F32),
+    pltpu.VMEM((3, 8, SLAB, 128), BF16),
+    pltpu.VMEM((256, 512), BF16),
+    pltpu.VMEM((3, RING, 1024, 128), BF16),
+    pltpu.VMEM((3, 2, 512, 128), BF16),
+    pltpu.VMEM((3, 2, 1024, 128), BF16),
+    pltpu.VMEM((3, 1024, 128), F32),
+    pltpu.VMEM((3, RING, 256, 128), BF16),
+    pltpu.VMEM((3, 3, 256, 128), BF16),
+]
+
+
+def keys_of(block_dest, block_row):
+    face, tile = block_dest >> 4, block_dest & 15
+    pos = {"x": tile & 3, "y": face >> 1, "z": tile >> 2}
+    out = []
+    for first, second, third in PARTS:
+        high = pos[first] * 2 + (face & 1)
+        low = pos[second] * 64 + pos[third] * 16 + block_row
+        both = jnp.stack([high, low])[:, None, :]
+        both = jnp.broadcast_to(both, (2, 8, ITEMS)).reshape(16, ITEMS)
+        out.append(jnp.concatenate([both, both], axis=1))
+    return jnp.stack(out).astype(BF16)
+
+
+def regrid_kernel(met_ref, weight_ref, key_ref, mx_ref, send, recv, *scratch):
+    at = whereabouts()
+    barrier, count = greet(at)
+    contributions(met_ref, weight_ref, scratch[0])
+    pl.semaphore_wait(barrier, count)
+    copies = Copies(send, recv)
+    regrid(at, copies, met_ref, weight_ref, key_ref, mx_ref, *scratch)
+    copies.sent()
+    mx_ref[768:1024, :] = jnp.zeros((256, 128), F32)
+
+
+def regrid_call(met_src, weights, keys):
+    vmem = pl.BlockSpec(memory_space=pltpu.VMEM)
+    return pl.pallas_call(
+        regrid_kernel,
+        out_shape=jax.ShapeDtypeStruct((1024, 128), F32),
+        in_specs=[vmem] * 3,
+        out_specs=vmem,
+        scratch_shapes=[pltpu.SemaphoreType.DMA((66,)), pltpu.SemaphoreType.DMA((66,))] + REGRID_SCRATCH,
+        compiler_params=pltpu.CompilerParams(collective_id=0, has_side_effects=True, vmem_limit_bytes=50 << 20),
+        name="regrid",
+    )(met_src, weights, keys)
+
+
 ADV_STEPS = 2
 
 
@@ -26,46 +258,13 @@
     return block
 
 
-def deliver(packed, slot_label):
-    arrived, labels = (
-        lax.all_to_all(packed, ("face", "tile"), split_axis=0, concat_axis=0, tiled=True),
-        lax.all_to_all(slot_label, ("face", "tile"), split_axis=0, concat_axis=0, tiled=True),
-    )
-    return (arrived, labels)
-
-
 def local(met_src, intersection_weights, block_dest, block_row, tracers, rate_coef, photo_coef):
-    n_face = lax.axis_size("face")
-    n_tile = lax.axis_size("tile")
-    owner_count = n_face * n_tile
-    blocks, levfields, cell_count = met_src.shape
+    levfields = met_src.shape[1]
     nfields = rate_coef.shape[1]
     levels = levfields // nfields
-    rows_x = tracers.shape[2]
-    slot_count = owner_count * CAP
-    owners = jnp.arange(owner_count, dtype=jnp.int32)
-    matches = (block_dest[:, None] == owners[None, :]).astype(jnp.int32)
-    earlier_count = jnp.cumsum(matches, axis=0) - 1
-    own_rank = jnp.sum(earlier_count * matches, axis=1)
-    position = block_dest * CAP + own_rank
-    placer = (jnp.arange(slot_count, dtype=jnp.int32)[:, None] == position[None, :]).astype(
-        jnp.bfloat16
-    )
-    slot_label = (
-        jnp.dot(placer, (block_row + 1).astype(jnp.bfloat16), preferred_element_type=jnp.float32)
-        - 1.0
-    ).astype(jnp.bfloat16)
-    contrib = jnp.einsum(
-        "sfi,sij->sfj", met_src, intersection_weights, preferred_element_type=jnp.float32
-    ).astype(jnp.bfloat16)
-    payload = contrib.reshape(blocks, levfields * cell_count)
-    packed = jnp.dot(placer, payload, preferred_element_type=jnp.float32).astype(jnp.bfloat16)
-    arrived, labels = deliver(packed, slot_label)
-    received = arrived.reshape(slot_count, levfields, cell_count)
-    row_values = jnp.arange(rows_x).astype(jnp.bfloat16)
-    chooser = (labels[:, None] == row_values[None, :]).astype(jnp.bfloat16)
-    met_flat = jnp.einsum("rt,rfc->ftc", chooser, received, preferred_element_type=jnp.float32)
-    met_tile = met_flat.reshape(nfields, levels, rows_x, cell_count)
+    rows_x, cell_count = tracers.shape[2], tracers.shape[3]
+    mx = regrid_call(met_src, intersection_weights, keys_of(block_dest, block_row))
+    met_tile = mx[:768].reshape(nfields, levels, rows_x, cell_count)
     courant_x = 0.3 * jnp.tanh(met_tile[0])
     courant_y = 0.3 * jnp.tanh(met_tile[1])
     west_row = from_behind(courant_x[:, -1:, :], "face", 1)

time: 204 us -> 169 us (0.83)
  Pallas kernels: 0 us -> 42.7 us
  waiting for transfers between devices: 46.4 us -> 13.3 us
  local copies, waits for them, and re-layouts: 38.8 us -> 23.1 us
  starting transfers between devices: 32 us -> 17.5 us
  matrix products: 30 us -> 22 us
  other arithmetic: 55 us -> 48.5 us
    pallas_call x0 -> x1, Pallas kernels: none -> 42.7 us  [regrid_call(): pl.pallas_call(regrid_kernel, out_shape=jax.ShapeDtypeStruct((1024, 128),...]
    ppermute x4, waiting for transfers between devices: 30.8 us -> 0.01 us  [with_halo(): lax.ppermute(lax.slice_in_dim(block, 0, width, axis=dim), axis, backward)]
    all_to_all x2 -> x0, starting transfers between devices: 21.4 us -> none  [the longest x1 11.2 us: deliver(): lax.all_to_all(slot_label, ('face', 'tile'), split_axis=0, concat_axis=0,...]
    reshape x1 -> x0, local copies, waits for them, and re-layouts: 7.97 us -> none  [local(): received = arrived.reshape(slot_count, levfields, cell_count)]
    dot_general x4 -> x0, matrix products: 7.86 us -> none  [the longest x1 2.64 us: local(): jnp.dot(placer, payload, preferred_element_type=jnp.float32)]
    all_to_all x2 -> x0, local copies, waits for them, and re-layouts: 7.84 us -> none  [the longest x1 7.03 us: deliver(): lax.all_to_all(packed, ('face', 'tile'), split_axis=0, concat_axis=0, til...]
    ppermute x4, starting transfers between devices: 9.63 us -> 16.6 us  [with_halo(): lax.ppermute(lax.slice_in_dim(block, 0, width, axis=dim), axis, backward)]
    add x2, other arithmetic: 18.4 us -> 13.7 us  [local(): jnp.maximum(courant_ye, 0.0) * lower_y]
  transfers between devices with their start and end apart: 12 -> 10, of which waited for: 7 -> 2; matrix products, arithmetic and copies ran while one was open for 23% -> 8% of each run, Pallas kernels for 0% -> 25%
where the time goes in v1:
time: 169 us; the launch traced here: 168 us
  other arithmetic  48.5 us (29%)
  Pallas kernels  42.7 us (25%)
  local copies, waits for them, and re-layouts  23.1 us (14%)
  matrix products  22 us (13%)
  starting transfers between devices  17.5 us (10%)
  waiting for transfers between devices  13.3 us (8%)
    pallas_call x1, Pallas kernels, regrid_call(): pl.pallas_call(regrid_kernel, out_shape=jax.ShapeDtypeStruct((1024, 128),...  42.7 us
    dot_general x1, matrix products, local(): jnp.einsum('sf,flxy->slxy', rate_coef, met_tile, precision=lax.Precision....  22 us
    unnamed x22, local copies, waits for them, and re-layouts  20.2 us
    sub x1, other arithmetic, local(): padded[:, :, 1:-1, 1:-1] - (flux_x[:, :, 1:, :] - flux_x[:, :, :-1, :])  19.2 us
    ppermute x4, starting transfers between devices, with_halo(): lax.ppermute(lax.slice_in_dim(block, 0, width, axis=dim), axis, backward)  16.6 us
    add x2, other arithmetic, local(): jnp.maximum(courant_ye, 0.0) * lower_y  13.7 us
    add x2, other arithmetic, local(): jnp.maximum(courant_xe, 0.0) * lower_x  12.4 us
    ppermute x4, waiting for transfers between devices, with_halo(): lax.ppermute(lax.slice_in_dim(block, block.shape[dim] - width, None, axis...  6.79 us
  transfers between devices with their start and end apart: 10, of which 2 were waited for; matrix products, arithmetic and copies ran while one was open for 8% of the time, Pallas kernels for 25%

profile of v1, /device:TPU:0, one launch (start us, length us, event | category | flops | bytes accessed | tf_op | source)
XLA Modules:
  0.0 168.1 jit_solution(2189263358479922252)
XLA Ops:
  0.6 0.0 copy-start
  0.7 10.1 %copy.13 = f32[250,4,16,128]{0,3,2,1:T(8,128)} copy(f32[250,4,16,128]{3,2,1,0:T(8,128)} %param.11) | data formatting | bytes 16384000 | tf_op args[4]
  10.8 1.4 fusion.30
  12.2 0.0 collective-permute-start.1
  12.3 2.9 %collective-permute-start.2 = (f32[250,4,1,128]{0,3,2,1:T(8,128)S(1)}, f32[250,4,1,128]{0,3,2,1:T(8,128)S(1)}, u32[]{:S(2)}, u32[]{:S(2)}) collective-permute-start(f32[250,4,1,128]{0,3,2,1:T(8,128)S(1)} %get-tuple-element.11), channel_id=1, source_target_pairs={{16,0},{32,16},{48,32},{64,48},{80,64},{96,80},{112,96},{0,112},{1... | collective-permute-start | bytes 1536008 | tf_op jit(solution)/shard_map/ppermute | solution.py:256
  15.3 0.1 maximum_bitcast_fusion.2
  15.4 0.1 maximum_bitcast_fusion
  15.4 0.1 maximum_bitcast_fusion.1
  15.5 42.7 %regrid.1 = f32[1024,128]{1,0:T(8,128)S(1)} custom-call(bf16[64,48,128]{2,1,0:T(8,128)(2,1)S(1)} %copy-done.2, bf16[64,128,128]{2,1,0:T(8,128)(2,1)S(1)} %copy-done.1, bf16[3,16,128]{2,1,0:T(8,128)(2,1)S(1)} %pad_maximum_fusion.20.key_ref), custom_call_target="tpu_custom_call" | custom-call | tf_op jit(solution)/shard_map/regrid/pallas_call | solution.py:228
  58.3 0.1 slice.127
  58.4 0.8 collective-permute-start.3
  59.2 0.0 collective-permute-start
  59.2 6.5 %collective-permute-done.3 = f32[4,16,1]{2,1,0:T(8,128)S(1)} collective-permute-done((f32[4,16,1]{2,1,0:T(8,128)S(1)}, f32[4,16,1]{2,1,0:T(8,128)S(1)}, u32[]{:S(2)}, u32[]{:S(2)}) %collective-permute-start.3) | collective-permute-done | bytes 288 | tf_op jit(solution)/shard_map/ppermute | solution.py:244
  65.6 0.1 fusion.17
  65.8 1.5 pad_maximum_fusion.17
  67.3 0.1 collective-permute-start.4
  67.4 5.3 %collective-permute-start.5 = (f32[250,4,18,1]{0,3,2,1:T(1,128)S(1)}, f32[250,4,18,1]{0,3,2,1:T(1,128)S(1)}, u32[]{:S(2)}, u32[]{:S(2)}) collective-permute-start(f32[250,4,18,1]{0,3,2,1:T(1,128)S(1)} %get-tuple-element.7), channel_id=1, source_target_pairs={{1,0},{2,1},{3,2},{4,3},{5,4},{6,5},{7,6},{8,7},{9,8},{10,9},{11,1... | collective-permute-start | bytes 216008 | tf_op jit(solution)/shard_map/ppermute | solution.py:256
  72.7 6.2 %fusion.6 = f32[250,4,17,128]{0,3,2,1:T(8,128)} fusion(f32[250,4,16,128]{0,3,2,1:T(8,128)S(1)} %bitcast.38, f32[250,4,1,128]{0,3,2,1:T(8,128)S(1)} %collective-permute-done.1, f32[250,4,1,128]{0,3,2,1:T(8,128)S(1)} %collective-permute-done.2, f32[4,17,128]{2,1,0:T(8,128)S(1)} %get-tuple-element.18, f32[4,17,128]{2,1,0:T(8,128)S(1)} %get-tuple-element.17), kind=kLoop, calls=%fused_computation.20 | loop fusion | flops 10880000 | bytes 17989632 | tf_op jit(solution)/shard_map/add | solution.py:279
  78.9 6.9 %fusion.4 = f32[250,4,16,129]{0,3,2,1:T(8,128)} fusion(f32[250,4,18,1]{0,3,2,1:T(1,128)S(1)} %collective-permute-done.5, f32[250,4,1,128]{0,3,2,1:T(8,128)S(1)} %collective-permute-done.2, f32[250,4,16,128]{0,3,2,1:T(8,128)S(1)} %bitcast.38, f32[250,4,1,128]{0,3,2,1:T(8,128)S(1)} %collective-permute-done.1, f32[250,4,18,1]{0,3,2,1:T(1,128)S(1)} %collective-permute-done.4, ...), kind=kLoop, calls=%fused_computation.12 | loop fusion | flops 18576000 | bytes 17682048 | tf_op jit(solution)/shard_map/add | solution.py:282
  85.7 19.2 %fusion.12 = f32[250,4,16,128]{0,3,2,1:T(8,128)} fusion(f32[250,4,16,129]{0,3,2,1:T(8,128)} %fusion.4, f32[250,4,16,128]{0,3,2,1:T(8,128)} %copy.13, f32[250,4,17,128]{0,3,2,1:T(8,128)} %fusion.6), kind=kLoop, calls=%fused_computation.32 | loop fusion | flops 8192000 | bytes 49152000 | tf_op jit(solution)/shard_map/sub | solution.py:284
  105.0 1.4 fusion.29
  106.4 0.0 collective-permute-start.6
  106.4 2.9 %collective-permute-start.7 = (f32[250,4,1,128]{0,3,2,1:T(8,128)S(1)}, f32[250,4,1,128]{0,3,2,1:T(8,128)S(1)}, u32[]{:S(2)}, u32[]{:S(2)}) collective-permute-start(f32[250,4,1,128]{0,3,2,1:T(8,128)S(1)} %get-tuple-element.9), channel_id=1, source_target_pairs={{16,0},{32,16},{48,32},{64,48},{80,64},{96,80},{112,96},{0,112},{1... | collective-permute-start | bytes 1536008 | tf_op jit(solution)/shard_map/ppermute | solution.py:256
  109.4 0.0 copy-start.4
  109.4 6.8 %collective-permute-done.6 = f32[250,4,1,128]{0,3,2,1:T(8,128)S(1)} collective-permute-done((f32[250,4,1,128]{0,3,2,1:T(8,128)S(1)}, f32[250,4,1,128]{0,3,2,1:T(8,128)S(1)}, u32[]{:S(2)}, u32[]{:S(2)}) %collective-permute-start.6) | collective-permute-done | bytes 512032 | tf_op jit(solution)/shard_map/ppermute | solution.py:253
  116.2 1.3 pad_maximum_fusion.14
  117.5 0.1 collective-permute-start.8
  117.6 5.3 %collective-permute-start.9 = (f32[250,4,18,1]{0,3,2,1:T(1,128)S(1)}, f32[250,4,18,1]{0,3,2,1:T(1,128)S(1)}, u32[]{:S(2)}, u32[]{:S(2)}) collective-permute-start(f32[250,4,18,1]{0,3,2,1:T(1,128)S(1)} %get-tuple-element.5), channel_id=1, source_target_pairs={{1,0},{2,1},{3,2},{4,3},{5,4},{6,5},{7,6},{8,7},{9,8},{10,9},{11,1... | collective-permute-start | bytes 216008 | tf_op jit(solution)/shard_map/ppermute | solution.py:256
  123.0 6.2 %fusion.7 = f32[250,4,17,128]{0,3,2,1:T(8,128)} fusion(f32[250,4,16,128]{0,3,2,1:T(8,128)S(1)} %copy-done.3, f32[250,4,1,128]{0,3,2,1:T(8,128)S(1)} %collective-permute-done.6, f32[250,4,1,128]{0,3,2,1:T(8,128)S(1)} %collective-permute-done.7, f32[4,17,128]{2,1,0:T(8,128)S(1)} %get-tuple-element.18, f32[4,17,128]{2,1,0:T(8,128)S(1)} %get-tuple-element.17), kind=kLoop, calls=%fused_computation.23 | loop fusion | flops 10880000 | bytes 17989632 | tf_op jit(solution)/shard_map/add | solution.py:279
  129.2 6.9 %fusion.1 = f32[250,4,16,129]{0,3,2,1:T(8,128)} fusion(f32[250,4,18,1]{0,3,2,1:T(1,128)S(1)} %collective-permute-done.9, f32[250,4,1,128]{0,3,2,1:T(8,128)S(1)} %collective-permute-done.7, f32[250,4,16,128]{0,3,2,1:T(8,128)S(1)} %copy-done.3, f32[250,4,1,128]{0,3,2,1:T(8,128)S(1)} %collective-permute-done.6, f32[250,4,18,1]{0,3,2,1:T(1,128)S(1)} %collective-permute-done.8, ...), kind=kLoop, calls=%fused_computation.3 | loop fusion | flops 18576000 | bytes 17682048 | tf_op jit(solution)/shard_map/add | solution.py:282
  136.0 22.0 %fusion.9 = f32[250,4,16,128]{0,3,2,1:T(8,128)} fusion(f32[250,4,16,129]{0,3,2,1:T(8,128)} %fusion.1, f32[250,4,16,128]{0,3,2,1:T(8,128)} %fusion.12, f32[250,4,17,128]{0,3,2,1:T(8,128)} %fusion.7, f32[4,16,128]{2,1,0:T(8,128)S(1)} %fusion.14, f32[250]{0:T(256)S(1)} %copy-done.7, f32[12,4,16,128]{3,2,1,0:T(8,128)S(1)} %bitcast.39, f32[250,12]{0,1:T(8,128)S(1)} %copy-done), kind=kOutput, calls=%fused_computation.26 | convolution fusion | flops 323584000 | bytes 49590984 | tf_op jit(solution)/shard_map/sf,flxy->slxy/dot_general | solution.py:291
  158.1 10.0 %copy.16 = f32[250,4,16,128]{3,2,1,0:T(8,128)} copy(f32[250,4,16,128]{0,3,2,1:T(8,128)} %fusion.9) | data formatting | bytes 16384000
  (39 shorter events, 0.2 us)
Async XLA Ops:
  0.6 135.4 %copy-start = (f32[250,12]{0,1:T(8,128)S(1)}, f32[250,12]{0,1:T(8,128)}, u32[]{:S(2)}) copy-start(f32[250,12]{0,1:T(8,128)} %param.12) | copy-start | bytes 36004
  0.6 14.6 %copy-start.5 = (s32[64]{0:T(128)S(1)}, s32[64]{0:T(128)}, u32[]{:S(2)}) copy-start(s32[64]{0:T(128)} %param.10) | copy-start | bytes 772
  0.7 14.6 %copy-start.6 = (s32[64]{0:T(128)S(1)}, s32[64]{0:T(128)}, u32[]{:S(2)}) copy-start(s32[64]{0:T(128)} %param.9) | copy-start | bytes 772
  0.7 14.9 %copy-start.1 = (bf16[64,128,128]{2,1,0:T(8,128)(2,1)S(1)}, bf16[64,128,128]{2,1,0:T(8,128)(2,1)}, u32[]{:S(2)}) copy-start(bf16[64,128,128]{2,1,0:T(8,128)(2,1)} %weight_ref.1) | copy-start | bytes 6291460
  0.7 14.9 %copy-start.2 = (bf16[64,48,128]{2,1,0:T(8,128)(2,1)S(1)}, bf16[64,48,128]{2,1,0:T(8,128)(2,1)}, u32[]{:S(2)}) copy-start(bf16[64,48,128]{2,1,0:T(8,128)(2,1)} %met_ref.1) | copy-start | bytes 2359300
  10.8 61.9 %slice-start = ((s8[8388608]{0:T(1024)(128)(4,1)}), s8[4194304]{0:T(1024)(128)(4,1)S(1)}, s32[]{:S(2)}) async-start(s8[8388608]{0:T(1024)(128)(4,1)} %bitcast.37), calls=%async_computation | async-start | bytes 8388608
  12.2 53.5 %collective-permute-start.1 = (f32[250,4,1,128]{0,3,2,1:T(8,128)S(1)}, f32[250,4,1,128]{0,3,2,1:T(8,128)S(1)}, u32[]{:S(2)}, u32[]{:S(2)}) collective-permute-start(f32[250,4,1,128]{0,3,2,1:T(8,128)S(1)} %get-tuple-element.10), channel_id=1, source_target_pairs={{0,16},{16,32},{32,48},{48,64},{64,80},{80,96},{96,112},{112,0},{1... | collective-permute-start | bytes 1536008 | tf_op jit(solution)/shard_map/ppermute | solution.py:253
  12.3 53.5 %collective-permute-start.2 = (f32[250,4,1,128]{0,3,2,1:T(8,128)S(1)}, f32[250,4,1,128]{0,3,2,1:T(8,128)S(1)}, u32[]{:S(2)}, u32[]{:S(2)}) collective-permute-start(f32[250,4,1,128]{0,3,2,1:T(8,128)S(1)} %get-tuple-element.11), channel_id=1, source_target_pairs={{16,0},{32,16},{48,32},{64,48},{80,64},{96,80},{112,96},{0,112},{1... | collective-permute-start | bytes 1536008 | tf_op jit(solution)/shard_map/ppermute | solution.py:256
  58.4 7.2 %collective-permute-start.3 = (f32[4,16,1]{2,1,0:T(8,128)S(1)}, f32[4,16,1]{2,1,0:T(8,128)S(1)}, u32[]{:S(2)}, u32[]{:S(2)}) collective-permute-start(f32[4,16,1]{2,1,0:T(8,128)S(1)} %slice.127), channel_id=1, source_target_pairs={{0,1},{1,2},{2,3},{3,4},{4,5},{5,6},{6,7},{7,8},{8,9},{9,10},{10,1... | collective-permute-start | bytes 776 | tf_op jit(solution)/shard_map/ppermute | solution.py:244
  59.2 6.6 %collective-permute-start = (f32[4,1,128]{2,1,0:T(1,128)S(1)}, f32[4,1,128]{2,1,0:T(1,128)S(1)}, u32[]{:S(2)}, u32[]{:S(2)}) collective-permute-start(f32[4,1,128]{2,1,0:T(1,128)S(1)} %slice.122), channel_id=1, source_target_pairs={{0,16},{16,32},{32,48},{48,64},{64,80},{80,96},{96,112},{112,0},{1... | collective-permute-start | bytes 6152 | tf_op jit(solution)/shard_map/ppermute | solution.py:244
  65.8 6.9 %slice-start.1 = ((s8[8388608]{0:T(1024)(128)(4,1)}), s8[4194304]{0:T(1024)(128)(4,1)S(1)}, s32[]{:S(2)}) async-start(s8[8388608]{0:T(1024)(128)(4,1)} %bitcast.37), calls=%async_computation.1 | async-start | bytes 8388608
  67.3 11.6 %collective-permute-start.4 = (f32[250,4,18,1]{0,3,2,1:T(1,128)S(1)}, f32[250,4,18,1]{0,3,2,1:T(1,128)S(1)}, u32[]{:S(2)}, u32[]{:S(2)}) collective-permute-start(f32[250,4,18,1]{0,3,2,1:T(1,128)S(1)} %get-tuple-element.6), channel_id=1, source_target_pairs={{0,1},{1,2},{2,3},{3,4},{4,5},{5,6},{6,7},{7,8},{8,9},{9,10},{10,1... | collective-permute-start | bytes 216008 | tf_op jit(solution)/shard_map/ppermute | solution.py:253
  67.4 11.5 %collective-permute-start.5 = (f32[250,4,18,1]{0,3,2,1:T(1,128)S(1)}, f32[250,4,18,1]{0,3,2,1:T(1,128)S(1)}, u32[]{:S(2)}, u32[]{:S(2)}) collective-permute-start(f32[250,4,18,1]{0,3,2,1:T(1,128)S(1)} %get-tuple-element.7), channel_id=1, source_target_pairs={{1,0},{2,1},{3,2},{4,3},{5,4},{6,5},{7,6},{8,7},{9,8},{10,9},{11,1... | collective-permute-start | bytes 216008 | tf_op jit(solution)/shard_map/ppermute | solution.py:256
  105.0 18.0 %copy-start.3 = (f32[250,4,16,128]{0,3,2,1:T(8,128)S(1)}, f32[250,4,16,128]{0,3,2,1:T(8,128)}, u32[]{:S(2)}) copy-start(f32[250,4,16,128]{0,3,2,1:T(8,128)} %fusion.12) | copy-start | bytes 24576004
  106.4 9.8 %collective-permute-start.6 = (f32[250,4,1,128]{0,3,2,1:T(8,128)S(1)}, f32[250,4,1,128]{0,3,2,1:T(8,128)S(1)}, u32[]{:S(2)}, u32[]{:S(2)}) collective-permute-start(f32[250,4,1,128]{0,3,2,1:T(8,128)S(1)} %get-tuple-element.8), channel_id=1, source_target_pairs={{0,16},{16,32},{32,48},{48,64},{64,80},{80,96},{96,112},{112,0},{1... | collective-permute-start | bytes 1536008 | tf_op jit(solution)/shard_map/ppermute | solution.py:253
  106.4 9.8 %collective-permute-start.7 = (f32[250,4,1,128]{0,3,2,1:T(8,128)S(1)}, f32[250,4,1,128]{0,3,2,1:T(8,128)S(1)}, u32[]{:S(2)}, u32[]{:S(2)}) collective-permute-start(f32[250,4,1,128]{0,3,2,1:T(8,128)S(1)} %get-tuple-element.9), channel_id=1, source_target_pairs={{16,0},{32,16},{48,32},{64,48},{80,64},{96,80},{112,96},{0,112},{1... | collective-permute-start | bytes 1536008 | tf_op jit(solution)/shard_map/ppermute | solution.py:256
  109.4 26.6 %copy-start.4 = (f32[768,128]{1,0:T(8,128)}, f32[768,128]{1,0:T(8,128)S(1)}, u32[]{:S(2)}) copy-start(f32[768,128]{1,0:T(8,128)S(1)} %slice.96) | copy-start | bytes 1179652
  117.5 11.6 %collective-permute-start.8 = (f32[250,4,18,1]{0,3,2,1:T(1,128)S(1)}, f32[250,4,18,1]{0,3,2,1:T(1,128)S(1)}, u32[]{:S(2)}, u32[]{:S(2)}) collective-permute-start(f32[250,4,18,1]{0,3,2,1:T(1,128)S(1)} %get-tuple-element.4), channel_id=1, source_target_pairs={{0,1},{1,2},{2,3},{3,4},{4,5},{5,6},{6,7},{7,8},{8,9},{9,10},{10,1... | collective-permute-start | bytes 216008 | tf_op jit(solution)/shard_map/ppermute | solution.py:253
  117.6 11.5 %collective-permute-start.9 = (f32[250,4,18,1]{0,3,2,1:T(1,128)S(1)}, f32[250,4,18,1]{0,3,2,1:T(1,128)S(1)}, u32[]{:S(2)}, u32[]{:S(2)}) collective-permute-start(f32[250,4,18,1]{0,3,2,1:T(1,128)S(1)} %get-tuple-element.5), channel_id=1, source_target_pairs={{1,0},{2,1},{3,2},{4,3},{5,4},{6,5},{7,6},{8,7},{9,8},{10,9},{11,1... | collective-permute-start | bytes 216008 | tf_op jit(solution)/shard_map/ppermute | solution.py:256
  129.1 6.9 %copy-start.7 = (f32[250]{0:T(256)S(1)}, f32[250]{0:T(256)}, u32[]{:S(2)}) copy-start(f32[250]{0:T(256)} %param.13) | copy-start | bytes 3004

commit v2 on v1

--- a/solution.py
+++ b/solution.py
@@ -35,7 +35,7 @@
 
 class Copies:
     def __init__(self, send, recv):
-        self.send, self.recv, self.made = send, recv, {}
+        self.send, self.recv, self.made, self.over = send, recv, {}, set()
 
     def start(self, index, src, dst, there):
         copy = pltpu.make_async_remote_copy(
@@ -43,7 +43,7 @@
             dst_ref=dst,
             send_sem=self.send.at[index],
             recv_sem=self.recv.at[index],
-            device_id=device(there),
+            device_id=device(there) if isinstance(there, dict) else there,
             device_id_type=MESH,
         )
         copy.start()
@@ -53,12 +53,16 @@
         for index in indices:
             self.made[index].wait_recv()
 
+    def sent_of(self, *indices):
+        for index in indices:
+            self.made[index].wait_send()
+            self.over.add(index)
+
     def sent(self):
-        for copy in self.made.values():
-            copy.wait_send()
-
-
-def regrid(at, copies, met_ref, weight_ref, key_ref, mx_ref, cs, gath, mask, part_sum, relay, ring_in, full, cut_sum, last_in):
+        self.sent_of(*[index for index in self.made if index not in self.over])
+
+
+def regrid(at, copies, met_ref, weight_ref, key_ref, mx_ref, cs, gath, mask, part_sum, relay, ring_in, full, cut_sum, last_in, meanwhile):
     me = {p: at[dims[0]] * 2 + at["c"] for p, dims in enumerate(PARTS)}
     low, high = pl.ds(0, CUT), pl.ds(CUT, SLAB - CUT)
 
@@ -86,6 +90,7 @@
         pass_on(p, None, low, 3, 6, moved(at, "c", 1))
         pass_on(p, 2, high, 1, 7, moved(at, first, 3))
         pass_on(p, None, high, 1, 8, moved(at, "c", 1))
+    meanwhile()
     for p, (first, second, third) in enumerate(PARTS):
         pass_on(p, 1, high, 3, 9, moved(at, "c", 1))
         pass_on(p, 3, low, 1, 10, moved(at, "c", 1))
@@ -178,11 +183,12 @@
             cs[pl.ds(s, 48, stride=ITEMS), :] = jnp.dot(met_ref[s], weight_ref[s], preferred_element_type=F32)
 
 
-def greet(at):
+def greet(at, near):
     barrier = pltpu.get_barrier_semaphore()
     peers = [moved(at, dim, by) for dim in ("x", "y", "z") for by in (1, 2, 3)] + [moved(at, "c", 1)]
+    peers = [device(there) for there in peers] + [near[side] for side in "nsew"]
     for there in peers:
-        pl.semaphore_signal(barrier, inc=1, device_id=device(there), device_id_type=MESH)
+        pl.semaphore_signal(barrier, inc=1, device_id=there, device_id_type=MESH)
     return barrier, len(peers)
 
 
@@ -212,102 +218,288 @@
     return jnp.stack(out).astype(BF16)
 
 
-def regrid_kernel(met_ref, weight_ref, key_ref, mx_ref, send, recv, *scratch):
-    at = whereabouts()
-    barrier, count = greet(at)
-    contributions(met_ref, weight_ref, scratch[0])
+SPECIES = 256
+HALO_COPIES = 66
+
+
+def lanes_of(shape, dim):
+    return lax.broadcasted_iota(jnp.int32, shape, dim)
+
+
+def edge_picker(pick):
+    row, lane = lanes_of((128, 128), 0), lanes_of((128, 128), 1)
+    for r in range(16):
+        east = jnp.logical_and(row == 127, lane == 2 * r)
+        west = jnp.logical_and(row == 0, lane == 2 * r + 1)
+        pick[r * 128 : (r + 1) * 128, :] = jnp.where(jnp.logical_or(east, west), 1.0, 0.0).astype(BF16)
+
+
+def picked_edges(narrow, pick, l):
+    rows = jnp.concatenate([narrow[l, r] for r in range(16)], axis=1)
+    return jnp.dot(rows, pick[...], preferred_element_type=F32).astype(BF16)
+
+
+def neighbours():
+    face, tile = lax.axis_index("face"), lax.axis_index("tile")
+    return {
+        "n": (lax.rem(face + 1, 8), tile),
+        "s": (lax.rem(face + 7, 8), tile),
+        "e": (face, lax.rem(tile + 1, 16)),
+        "w": (face, lax.rem(tile + 15, 16)),
+    }
+
+
+def start_tracers(tracer_ref, amount, load):
+    count = tracer_ref.shape[0]
+    copies = []
+    for lr in range(64):
+        copy = pltpu.make_async_copy(
+            tracer_ref.at[:, lr, 0], amount.at[lr // 16, lr % 16 + 1, pl.ds(0, count)], load.at[lr]
+        )
+        copy.start()
+        copies.append(copy)
+    return copies
+
+
+def first_halos(near, copies, loads, amount, narrow, pick, edges, row_in, edge_in):
+    for copy in loads:
+        copy.wait()
+    count = 250
+
+    @pl.loop(0, 64)
+    def _(lr):
+        narrow[lr // 16, lax.rem(lr, 16)] = amount[lr // 16, lax.rem(lr, 16) + 1].astype(BF16)
+
+    copies.start(HALO_COPIES + 0, narrow.at[:, 15], row_in.at[0, 0], near["n"])
+    copies.start(HALO_COPIES + 1, narrow.at[:, 0], row_in.at[0, 1], near["s"])
+
+    @pl.loop(0, 4)
+    def _(l):
+        edges[0, l] = picked_edges(narrow, pick, l)
+
+    copies.start(HALO_COPIES + 2, edges.at[0], edge_in.at[0, 0], near["e"])
+    copies.start(HALO_COPIES + 3, edges.at[0], edge_in.at[0, 1], near["w"])
+
+
+def coefficients(near, copies, mx_ref, courant, courant_in, shifted, coef, band):
+    courant[0] = 0.3 * jnp.tanh(mx_ref[0:64, :])
+    courant[1] = 0.3 * jnp.tanh(mx_ref[64:128, :])
+    copies.start(HALO_COPIES + 4, courant.at[0], courant_in.at[0], near["n"])
+    copies.start(HALO_COPIES + 5, courant.at[1], courant_in.at[1], near["e"])
+
+    depth = jnp.zeros((16, 128), F32)
+    for l in range(4):
+        value = mx_ref[128 + l * 16 : 144 + l * 16, :]
+        depth = depth + (jnp.maximum(value, 0.0) + jnp.log1p(jnp.exp(-jnp.abs(value))))
+        mx_ref[768 + l * 16 : 784 + l * 16, :] = jnp.exp(-depth)
+    mx_ref[832:1024, :] = jnp.zeros((192, 128), F32)
+
+    row, lane = lanes_of((128, 128), 0), lanes_of((128, 128), 1)
+    from_west = jnp.where(row == lane - 1, 1.0, 0.0)
+    from_east = jnp.where(row == lane + 1, 1.0, 0.0)
+    sub, edge = lanes_of((16, 128), 0), lanes_of((16, 128), 1)
+    copies.arrived(HALO_COPIES + 4, HALO_COPIES + 5)
+    for l in range(4):
+        rows = slice(l * 16, l * 16 + 16)
+        shifted[l, 8:24, :] = courant[0, rows, :]
+        shifted[l, 7:8, :] = courant_in[0, l * 16 + 15 : l * 16 + 16, :]
+        cx, cy = courant[0, rows, :], courant[1, rows, :]
+        behind_x = shifted[l, 7:23, :]
+        behind_y = jnp.where(edge == 0, pltpu.roll(courant_in[1, rows, :], 1, 1), pltpu.roll(cy, 1, 1))
+        coef[l, 0] = 1.0 - jnp.maximum(cx, 0.0) + jnp.minimum(behind_x, 0.0) - jnp.maximum(cy, 0.0) + jnp.minimum(behind_y, 0.0)
+        coef[l, 1] = jnp.maximum(behind_x, 0.0)
+        coef[l, 2] = -jnp.minimum(cx, 0.0)
+        west, east = jnp.maximum(behind_y, 0.0), -jnp.minimum(cy, 0.0)
+        for r in range(16):
+            w, e = west[r : r + 1, :], east[r : r + 1, :]
+            band[l, r, 0:128, :] = (from_west * w + from_east * e).astype(BF16)
+            k = 2 * r % 16
+            ends = jnp.where(jnp.logical_and(sub == k, edge == 0), w, jnp.where(jnp.logical_and(sub == k + 1, edge == 127), e, 0.0))
+            other = 128 + 16 * (1 - r // 8)
+            band[l, r, 128 + 16 * (r // 8) : 144 + 16 * (r // 8), :] = ends.astype(BF16)
+            band[l, r, other : other + 16, :] = jnp.zeros((16, 128), BF16)
+
+
+def advance(source, target, narrow, side, coef, band, row_in, edge_in, step, l, keep):
+    source[l, 0] = row_in[step, 0, l].astype(F32)
+    source[l, 17] = row_in[step, 1, l].astype(F32)
+    even = lax.rem(lanes_of((SPECIES, 128), 1), 2) == 0
+    side[...] = jnp.where(even, edge_in[step, 0, l].astype(F32), edge_in[step, 1, l].astype(F32)).astype(BF16)
+
+    @pl.loop(0, 16)
+    def _(r):
+        lhs = jnp.concatenate([narrow[l, r], side[...]], axis=1)
+        across = jnp.dot(lhs, band[l, r], preferred_element_type=F32)
+        total = coef[l, 0, pl.ds(r, 1), :] * source[l, r + 1] + coef[l, 1, pl.ds(r, 1), :] * source[l, r]
+        total = total + coef[l, 2, pl.ds(r, 1), :] * source[l, r + 2] + across
+        target[l, r + 1] = total
+        if keep:
+            narrow[l, r] = total.astype(BF16)
+
+
+def advect(near, copies, adv_ref, amount, middle, narrow, side, pick, edges, coef, band, row_in, edge_in, store):
+    copies.arrived(*[HALO_COPIES + k for k in range(4)])
+    copies.sent_of(HALO_COPIES + 0, HALO_COPIES + 1)
+    for l in range(4):
+        advance(amount, middle, narrow, side, coef, band, row_in, edge_in, 0, l, True)
+        base = HALO_COPIES + 6 + 4 * l
+        copies.start(base + 0, narrow.at[l, 15], row_in.at[1, 0, l], near["n"])
+        copies.start(base + 1, narrow.at[l, 0], row_in.at[1, 1, l], near["s"])
+        edges[1, l] = picked_edges(narrow, pick, l)
+        copies.start(base + 2, edges.at[1, l], edge_in.at[1, 0, l], near["e"])
+        copies.start(base + 3, edges.at[1, l], edge_in.at[1, 1, l], near["w"])
+    stores = []
+    for l in range(4):
+        base = HALO_COPIES + 6 + 4 * l
+        copies.arrived(*[base + k for k in range(4)])
+        advance(middle, amount, narrow, side, coef, band, row_in, edge_in, 1, l, False)
+        copy = pltpu.make_async_copy(amount.at[l, pl.ds(1, 16)], adv_ref.at[l], store.at[l])
+        copy.start()
+        stores.append(copy)
+    for copy in stores:
+        copy.wait()
+
+
+ADVECT_SCRATCH = [
+    pltpu.VMEM((4, 18, SPECIES, 128), F32),
+    pltpu.VMEM((4, 18, SPECIES, 128), F32),
+    pltpu.VMEM((4, 16, SPECIES, 128), BF16),
+    pltpu.VMEM((SPECIES, 128), BF16),
+    pltpu.VMEM((2048, 128), BF16),
+    pltpu.VMEM((2, 4, SPECIES, 128), BF16),
+    pltpu.VMEM((2, 2, 4, SPECIES, 128), BF16),
+    pltpu.VMEM((2, 2, 4, SPECIES, 128), BF16),
+    pltpu.VMEM((2, 64, 128), F32),
+    pltpu.VMEM((2, 64, 128), F32),
+    pltpu.VMEM((4, 24, 128), F32),
+    pltpu.VMEM((4, 3, 16, 128), F32),
+    pltpu.VMEM((4, 16, 256, 128), BF16),
+]
+COPIES = HALO_COPIES + 22
+
+
+def transport_kernel(met_ref, weight_ref, key_ref, tracer_ref, mx_ref, adv_ref, send, recv, load, store, *scratch):
+    cut = len(REGRID_SCRATCH)
+    regrid_scratch = scratch[:cut]
+    amount, middle, narrow, side, pick, edges, row_in, edge_in, courant, courant_in, shifted, coef, band = scratch[cut:]
+    at, near = whereabouts(), neighbours()
+    loads = start_tracers(tracer_ref, amount, load)
+    barrier, count = greet(at, near)
+    contributions(met_ref, weight_ref, regrid_scratch[0])
     pl.semaphore_wait(barrier, count)
     copies = Copies(send, recv)
-    regrid(at, copies, met_ref, weight_ref, key_ref, mx_ref, *scratch)
+
+    def meanwhile():
+        edge_picker(pick)
+
+        @pl.loop(0, 64)
+        def _(k):
+            band[k // 16, lax.rem(k, 16), 128:256, :] = jnp.zeros((128, 128), BF16)
+
+        first_halos(near, copies, loads, amount, narrow, pick, edges, row_in, edge_in)
+
+    regrid(at, copies, met_ref, weight_ref, key_ref, mx_ref, *regrid_scratch, meanwhile=meanwhile)
+    coefficients(near, copies, mx_ref, courant, courant_in, shifted, coef, band)
+    advect(near, copies, adv_ref, amount, middle, narrow, side, pick, edges, coef, band, row_in, edge_in, store)
     copies.sent()
-    mx_ref[768:1024, :] = jnp.zeros((256, 128), F32)
-
-
-def regrid_call(met_src, weights, keys):
-    vmem = pl.BlockSpec(memory_space=pltpu.VMEM)
+
+
+def transport_call(met_src, weights, keys, tracers):
+    vmem, anywhere = pl.BlockSpec(memory_space=pltpu.VMEM), pl.BlockSpec(memory_space=pl.ANY)
+    dma = pltpu.SemaphoreType.DMA
     return pl.pallas_call(
-        regrid_kernel,
-        out_shape=jax.ShapeDtypeStruct((1024, 128), F32),
-        in_specs=[vmem] * 3,
-        out_specs=vmem,
-        scratch_shapes=[pltpu.SemaphoreType.DMA((66,)), pltpu.SemaphoreType.DMA((66,))] + REGRID_SCRATCH,
-        compiler_params=pltpu.CompilerParams(collective_id=0, has_side_effects=True, vmem_limit_bytes=50 << 20),
-        name="regrid",
-    )(met_src, weights, keys)
-
-
-ADV_STEPS = 2
-
-
-def from_behind(shard, axis, by):
-    devices = lax.axis_size(axis)
-    return lax.ppermute(shard, axis, [(i, (i + by) % devices) for i in range(devices)])
-
-
-def with_halo(block, sides, width):
-    for axis, dim in sides:
-        count = lax.axis_size(axis)
-        forward = [(i, i + 1) for i in range(count - 1)]
-        forward.append((count - 1, 0))
-        backward = [(target, source) for source, target in forward]
-        low = lax.ppermute(
-            lax.slice_in_dim(block, block.shape[dim] - width, None, axis=dim), axis, forward
-        )
-        high = lax.ppermute(lax.slice_in_dim(block, 0, width, axis=dim), axis, backward)
-        block = jnp.concatenate([low, block, high], axis=dim)
-    return block
+        transport_kernel,
+        out_shape=(jax.ShapeDtypeStruct((1024, 128), F32), jax.ShapeDtypeStruct((4, 16, SPECIES, 128), F32)),
+        in_specs=[vmem] * 3 + [anywhere],
+        out_specs=(vmem, anywhere),
+        scratch_shapes=[dma((COPIES,)), dma((COPIES,)), dma((64,)), dma((4,))] + REGRID_SCRATCH + ADVECT_SCRATCH,
+        compiler_params=pltpu.CompilerParams(collective_id=0, has_side_effects=True, vmem_limit_bytes=60 << 20),
+        name="transport",
+    )(met_src, weights, keys, tracers)
+
+
+CHUNK = 4
+
+
+def chemistry_kernel(mx_ref, rate_ref, adv_ref, met_ref, out_ref, amount, result, load, store):
+    chunks = 64 // CHUNK
+    count = out_ref.shape[0]
+
+    def fetch(k):
+        rows = pl.ds(k * CHUNK, CHUNK)
+        return pltpu.make_async_copy(adv_ref.at[rows], amount.at[rows], load.at[k])
+
+    def put(lr):
+        return pltpu.make_async_copy(result.at[lr, pl.ds(0, count)], out_ref.at[:, lr, 0], store.at[lr])
+
+    for k in range(chunks):
+        fetch(k).start()
+    met_ref[...] = mx_ref[0:768, :]
+
+    def fields(lr):
+        value = mx_ref[pl.ds(lr, 16, stride=64), :]
+        m1 = value.astype(BF16)
+        rest = value - m1.astype(F32)
+        m2 = rest.astype(BF16)
+        m3 = (rest - m2.astype(F32)).astype(BF16)
+        return jnp.concatenate([m1, m2, m3, m1, m2, m1], axis=0)
+
+    @pl.loop(0, chunks)
+    def _(k):
+        fetch(k).wait()
+        for pair in range(CHUNK // 2):
+            lr = k * CHUNK + 2 * pair
+            rhs = jnp.concatenate([fields(lr), fields(lr + 1)], axis=1)
+            exponent = jnp.dot(rate_ref[...], rhs, preferred_element_type=F32)
+            loss = jnp.maximum(exponent, 0.0) + jnp.log1p(jnp.exp(-jnp.abs(exponent)))
+            for side in range(2):
+                result[lr + side] = amount[lr + side] / (1.0 + loss[:, side * 128 : side * 128 + 128])
+                put(lr + side).start()
+
+    @pl.loop(0, 64)
+    def _(lr):
+        put(lr).wait()
+
+
+def chemistry_call(mx, rates, adv, count):
+    vmem, anywhere = pl.BlockSpec(memory_space=pltpu.VMEM), pl.BlockSpec(memory_space=pl.ANY)
+    dma = pltpu.SemaphoreType.DMA
+    return pl.pallas_call(
+        chemistry_kernel,
+        out_shape=(jax.ShapeDtypeStruct((768, 128), F32), jax.ShapeDtypeStruct((count, 64, 1, 128), F32)),
+        in_specs=[vmem, vmem, anywhere],
+        out_specs=(vmem, anywhere),
+        scratch_shapes=[pltpu.VMEM((64, SPECIES, 128), F32), pltpu.VMEM((64, SPECIES, 128), F32), dma((64 // CHUNK,)), dma((64,))],
+        compiler_params=pltpu.CompilerParams(vmem_limit_bytes=40 << 20),
+        name="chemistry",
+    )(mx, rates, adv)
+
+
+def rates_of(rate_coef, photo_coef):
+    both = jnp.concatenate([rate_coef, photo_coef[:, None]], axis=1)
+    both = jnp.pad(both, ((0, SPECIES - both.shape[0]), (0, 16 - both.shape[1])))
+    r1 = lax.reduce_precision(both, 8, 7)
+    r2 = lax.reduce_precision(both - r1, 8, 7)
+    r3 = both - r1 - r2
+    return jnp.concatenate([r1, r1, r1, r2, r2, r3], axis=1).astype(BF16)
 
 
 def local(met_src, intersection_weights, block_dest, block_row, tracers, rate_coef, photo_coef):
-    levfields = met_src.shape[1]
-    nfields = rate_coef.shape[1]
-    levels = levfields // nfields
-    rows_x, cell_count = tracers.shape[2], tracers.shape[3]
-    mx = regrid_call(met_src, intersection_weights, keys_of(block_dest, block_row))
-    met_tile = mx[:768].reshape(nfields, levels, rows_x, cell_count)
-    courant_x = 0.3 * jnp.tanh(met_tile[0])
-    courant_y = 0.3 * jnp.tanh(met_tile[1])
-    west_row = from_behind(courant_x[:, -1:, :], "face", 1)
-    south_column = from_behind(courant_y[:, :, -1:], "tile", 1)
-    courant_xe = jnp.concatenate([west_row, courant_x], axis=1)
-    courant_ye = jnp.concatenate([south_column, courant_y], axis=2)
-    amount = tracers
-    for substep in range(ADV_STEPS):
-        padded = with_halo(amount, (("face", 2), ("tile", 3)), 1)
-        lower_x = padded[:, :, 0 : rows_x + 1, 1:-1]
-        upper_x = padded[:, :, 1 : rows_x + 2, 1:-1]
-        flux_x = jnp.maximum(courant_xe, 0.0) * lower_x + jnp.minimum(courant_xe, 0.0) * upper_x
-        lower_y = padded[:, :, 1:-1, 0 : cell_count + 1]
-        upper_y = padded[:, :, 1:-1, 1 : cell_count + 2]
-        flux_y = jnp.maximum(courant_ye, 0.0) * lower_y + jnp.minimum(courant_ye, 0.0) * upper_y
-        amount = (
-            padded[:, :, 1:-1, 1:-1]
-            - (flux_x[:, :, 1:, :] - flux_x[:, :, :-1, :])
-            - (flux_y[:, :, :, 1:] - flux_y[:, :, :, :-1])
-        )
-    column_depth = jnp.cumsum(jax.nn.softplus(met_tile[2]), axis=0)
-    light = jnp.exp(-column_depth)
-    exponent = (
-        jnp.einsum("sf,flxy->slxy", rate_coef, met_tile, precision=lax.Precision.HIGHEST)
-        + photo_coef[:, None, None, None] * light[None]
-    )
-    species_out = amount / (1.0 + jax.nn.softplus(exponent))
-    return (met_tile, species_out)
+    species, levels, rows, cells = tracers.shape
+    keys = keys_of(block_dest, block_row)
+    rates = rates_of(rate_coef, photo_coef)
+    mx, adv = transport_call(met_src, intersection_weights, keys, tracers.reshape(species, levels * rows, 1, cells))
+    met, out = chemistry_call(mx, rates, adv.reshape(levels * rows, SPECIES, cells), species)
+    return met.reshape(-1, levels, rows, cells), out.reshape(species, levels, rows, cells)
 
 
 def solution(mesh):
+    split = P(("face", "tile"))
+    grid = P(None, None, "face", "tile")
     return jax.shard_map(
         local,
         mesh=mesh,
-        in_specs=(
-            P(("face", "tile"), None, None),
-            P(("face", "tile"), None, None),
-            P(("face", "tile")),
-            P(("face", "tile")),
-            P(None, None, "face", "tile"),
-            P(),
-            P(),
-        ),
-        out_specs=(P(None, None, "face", "tile"), P(None, None, "face", "tile")),
+        in_specs=(split, split, split, split, grid, P(), P()),
+        out_specs=(grid, grid),
         check_vma=False,
     )

time: 169 us -> 98.1 us (0.58)
  Pallas kernels: 42.7 us -> 89.9 us
  other arithmetic: 48.5 us -> 2.33 us
  matrix products: 22 us -> 0 us
  local copies, waits for them, and re-layouts: 23.1 us -> 4.73 us
  starting transfers between devices: 17.5 us -> 0 us
  waiting for transfers between devices: 13.3 us -> 0 us
    pallas_call x1 -> x2, Pallas kernels: 42.7 us -> 89.9 us  [the longest x1 79 us: transport_call(): pl.pallas_call(transport_kernel, out_shape=(jax.ShapeDtypeStruct((1024, 1...]
    add x4 -> x0, other arithmetic: 26.1 us -> none  [the longest x2 13.7 us: local(): jnp.maximum(courant_ye, 0.0) * lower_y]
    dot_general x1 -> x0, matrix products: 22 us -> none  [local(): jnp.einsum('sf,flxy->slxy', rate_coef, met_tile, precision=lax.Precision....]
    sub x1 -> x0, other arithmetic: 19.2 us -> none  [local(): padded[:, :, 1:-1, 1:-1] - (flux_x[:, :, 1:, :] - flux_x[:, :, :-1, :])]
    ppermute x10 -> x0, starting transfers between devices: 17.5 us -> none  [the longest x4 16.6 us: with_halo(): lax.ppermute(lax.slice_in_dim(block, 0, width, axis=dim), axis, backward)]
    unnamed x22 -> x4, local copies, waits for them, and re-layouts: 20.2 us -> 4.42 us
    ppermute x10 -> x0, waiting for transfers between devices: 13.3 us -> none  [the longest x4 6.79 us: with_halo(): lax.ppermute(lax.slice_in_dim(block, block.shape[dim] - width, None, axis...]
    slice x5 -> x0, local copies, waits for them, and re-layouts: 2.94 us -> none  [the longest x2 2.84 us: with_halo(): lax.slice_in_dim(block, block.shape[dim] - width, None, axis=dim)]
  transfers between devices with their start and end apart: 10 -> 0, of which waited for: 2 -> 0; matrix products, arithmetic and copies ran while one was open for 8% -> 0% of each run, Pallas kernels for 25% -> 0%
where the time goes in v2:
time: 98.1 us; the launch traced here: 97.6 us
  Pallas kernels  89.9 us (92%)
  local copies, waits for them, and re-layouts  4.73 us (5%)
  other arithmetic  2.33 us (2%)
    pallas_call x1, Pallas kernels, transport_call(): pl.pallas_call(transport_kernel, out_shape=(jax.ShapeDtypeStruct((1024, 1...  79 us
    pallas_call x1, Pallas kernels, chemistry_call(): pl.pallas_call(chemistry_kernel, out_shape=(jax.ShapeDtypeStruct((768, 12...  10.9 us
    unnamed x4, local copies, waits for them, and re-layouts  4.42 us

profile of v2, /device:TPU:0, one launch (start us, length us, event | category | flops | bytes accessed | tf_op | source)
XLA Modules:
  0.0 97.6 jit_solution(6313976098140105806)
XLA Ops:
  0.6 0.7 add_bitcast_fusion.4
  1.4 0.1 maximum_bitcast_fusion.2
  1.4 0.1 maximum_bitcast_fusion
  1.5 0.1 maximum_bitcast_fusion.1
  1.6 0.6 pad_maximum_fusion.1.key_ref
  2.2 0.7 pad_maximum_fusion
  3.0 0.1 copy.13
  3.1 0.2 concatenate.23.rate_ref
  3.3 79.0 %transport.1 = (f32[1024,128]{1,0:T(8,128)}, f32[4,16,256,128]{3,2,1,0:T(8,128)}) custom-call(bf16[64,48,128]{2,1,0:T(8,128)(2,1)} %met_ref.1, bf16[64,128,128]{2,1,0:T(8,128)(2,1)} %weight_ref.1, bf16[3,16,128]{2,1,0:T(8,128)(2,1)} %pad_maximum_fusion.1.key_ref, f32[250,64,1,128]{3,2,1,0:T(1,128)} %bitcast.30), custom_call_target="tpu_custom_call" | custom-call | tf_op jit(solution)/shard_map/transport/pallas_call | solution.py:410
  82.3 0.0 copy-start
  82.3 3.4 %copy-done = f32[4,16,256,128]{3,2,1,0:T(8,128)S(1)} copy-done((f32[4,16,256,128]{3,2,1,0:T(8,128)S(1)}, f32[4,16,256,128]{3,2,1,0:T(8,128)}, u32[]{:S(2)}) %copy-start) | copy-done | bytes 8388632
  85.7 0.0 copy-start.1
  85.7 1.0 %copy-done.1 = f32[1024,128]{1,0:T(8,128)S(1)} copy-done((f32[1024,128]{1,0:T(8,128)S(1)}, f32[1024,128]{1,0:T(8,128)}, u32[]{:S(2)}) %copy-start.1) | copy-done | bytes 524312
  86.7 10.9 %chemistry.1 = (f32[768,128]{1,0:T(8,128)}, f32[250,64,1,128]{3,2,1,0:T(1,128)}) custom-call(f32[1024,128]{1,0:T(8,128)S(1)} %copy-done.1, bf16[256,96]{1,0:T(8,128)(2,1)S(1)} %concatenate.23.rate_ref, f32[64,256,128]{2,1,0:T(8,128)S(1)} %bitcast.29), custom_call_target="tpu_custom_call" | custom-call | tf_op jit(solution)/shard_map/chemistry/pallas_call | solution.py:467
  (6 shorter events, 0.1 us)
Async XLA Ops:
  82.3 3.4 %copy-start = (f32[4,16,256,128]{3,2,1,0:T(8,128)S(1)}, f32[4,16,256,128]{3,2,1,0:T(8,128)}, u32[]{:S(2)}) copy-start(f32[4,16,256,128]{3,2,1,0:T(8,128)} %get-tuple-element.7) | copy-start | bytes 25165828
  85.7 1.0 %copy-start.1 = (f32[1024,128]{1,0:T(8,128)S(1)}, f32[1024,128]{1,0:T(8,128)}, u32[]{:S(2)}) copy-start(f32[1024,128]{1,0:T(8,128)} %get-tuple-element.6.mx_ref) | copy-start | bytes 1572868

commit v3 on v2

--- a/solution.py
+++ b/solution.py
@@ -14,7 +14,7 @@
 ITEMS = 64
 SLAB = 16 + 16 * ITEMS
 CUT = 16 + 8 * ITEMS
-PER_PART = 22
+PER_PART = 25
 
 
 def whereabouts():
@@ -62,117 +62,156 @@
         self.sent_of(*[index for index in self.made if index not in self.over])
 
 
-def regrid(at, copies, met_ref, weight_ref, key_ref, mx_ref, cs, gath, mask, part_sum, relay, ring_in, full, cut_sum, last_in, meanwhile):
-    me = {p: at[dims[0]] * 2 + at["c"] for p, dims in enumerate(PARTS)}
-    low, high = pl.ds(0, CUT), pl.ds(CUT, SLAB - CUT)
-
-    for p, (first, second, third) in enumerate(PARTS):
-        base, own = p * PER_PART, gath.at[p, me[p]]
-        nxt, prv, mate = moved(at, first, 1), moved(at, first, 3), moved(at, "c", 1)
-        gath[p, me[p], 0:16, :] = key_ref[p]
-        gath[p, me[p], 16:SLAB, :] = cs[p * 1024 : (p + 1) * 1024, :].astype(BF16)
-        copies.start(base + 0, own.at[low], own.at[low], nxt)
-        copies.start(base + 2, own.at[high], own.at[high], prv)
-        copies.start(base + 1, own.at[high], own.at[high], nxt)
-        copies.start(base + 3, own.at[low], own.at[low], prv)
-        copies.start(base + 4, own, own, mate)
-
-    def pass_on(p, wait, half, step, index, there):
-        base = p * PER_PART
-        slot = lax.rem(at[PARTS[p][0]] + step, RING) * 2 + at["c"]
-        ref = gath.at[p, slot, half]
-        if wait is not None:
-            copies.arrived(base + wait)
-        copies.start(base + index, ref, ref, there)
-
-    for p, (first, second, third) in enumerate(PARTS):
-        pass_on(p, 0, low, 3, 5, moved(at, first, 1))
-        pass_on(p, None, low, 3, 6, moved(at, "c", 1))
-        pass_on(p, 2, high, 1, 7, moved(at, first, 3))
-        pass_on(p, None, high, 1, 8, moved(at, "c", 1))
-    meanwhile()
-    for p, (first, second, third) in enumerate(PARTS):
-        pass_on(p, 1, high, 3, 9, moved(at, "c", 1))
-        pass_on(p, 3, low, 1, 10, moved(at, "c", 1))
-    for p, (first, second, third) in enumerate(PARTS):
-        pass_on(p, 5, low, 2, 11, moved(at, "c", 1))
-        pass_on(p, 7, high, 2, 12, moved(at, "c", 1))
-
-    lane = lax.broadcasted_iota(jnp.int32, (1, 128), 1)
-    rows = lax.broadcasted_iota(jnp.int32, (256, 128), 0).astype(F32)
-    h0, h1 = pl.ds(0, 512), pl.ds(512, 512)
-
-    for p, (first, second, third) in enumerate(PARTS):
-        base = p * PER_PART
-        copies.arrived(*[base + k for k in (4, 6, 8, 9, 10, 11, 12)])
-        mine = me[p].astype(F32)
+class Regrid:
+    def __init__(self, at, copies, key_ref, mx_ref, cs, gath, mask, part_sum, relay, ring_in, full, cut_sum, last_in):
+        self.at, self.copies, self.key_ref, self.mx_ref = at, copies, key_ref, mx_ref
+        self.cs, self.gath, self.mask, self.part_sum, self.relay = cs, gath, mask, part_sum, relay
+        self.ring_in, self.full, self.cut_sum, self.last_in = ring_in, full, cut_sum, last_in
+        self.me = [at[dims[0]] * 2 + at["c"] for dims in PARTS]
+        self.gather_rows = (pl.ds(0, CUT), pl.ds(CUT, SLAB - CUT))
+        self.sum_rows = (pl.ds(0, 512), pl.ds(512, 512))
+
+    def toward(self, p, k, by):
+        return moved(self.at, PARTS[p][k], by)
+
+    def arrived(self, p, *indices):
+        self.copies.arrived(*[p * PER_PART + k for k in indices])
+
+    def send(self, p, index, src, dst, there):
+        self.copies.start(p * PER_PART + index, src, dst, there)
+
+    def open(self, p):
+        own, mate = self.gath.at[p, self.me[p]], moved(self.at, "c", 1)
+        low, high = self.gather_rows
+        self.gath[p, self.me[p], 0:16, :] = self.key_ref[p]
+        self.gath[p, self.me[p], 16:SLAB, :] = self.cs[p * 1024 : (p + 1) * 1024, :].astype(BF16)
+        self.send(p, 0, own.at[low], own.at[low], self.toward(p, 0, 1))
+        self.send(p, 3, own.at[low], own.at[low], self.toward(p, 0, 3))
+        self.send(p, 2, own.at[high], own.at[high], self.toward(p, 0, 3))
+        self.send(p, 4, own, own, mate)
+
+    def pass_on(self, p, half, step, index, there):
+        slot = lax.rem(self.at[PARTS[p][0]] + step, RING) * 2 + self.at["c"]
+        ref = self.gath.at[p, slot, self.gather_rows[half]]
+        self.send(p, index, ref, ref, there)
+
+    def low_first(self, p):
+        mate, nxt = moved(self.at, "c", 1), self.toward(p, 0, 1)
+        own, high = self.gath.at[p, self.me[p]], self.gather_rows[1]
+        self.arrived(p, 0)
+        self.pass_on(p, 0, 3, 5, nxt)
+        self.send(p, 1, own.at[high], own.at[high], nxt)
+        self.pass_on(p, 0, 3, 6, mate)
+
+    def low_second(self, p):
+        self.arrived(p, 3)
+        self.pass_on(p, 0, 1, 10, moved(self.at, "c", 1))
+
+    def high_first(self, p):
+        mate, prv = moved(self.at, "c", 1), self.toward(p, 0, 3)
+        self.arrived(p, 2)
+        self.pass_on(p, 1, 1, 7, prv)
+        self.pass_on(p, 1, 1, 8, mate)
+
+    def low_third(self, p):
+        self.arrived(p, 5)
+        self.pass_on(p, 0, 2, 11, moved(self.at, "c", 1))
+
+    def high_rest(self, p):
+        mate = moved(self.at, "c", 1)
+        self.arrived(p, 1)
+        self.pass_on(p, 1, 3, 9, mate)
+        self.arrived(p, 7)
+        self.pass_on(p, 1, 2, 12, mate)
+
+    def build_mask(self, p):
+        gath, mask = self.gath, self.mask
+        lane = lax.broadcasted_iota(jnp.int32, (1, 128), 1)
+        rows = lax.broadcasted_iota(jnp.int32, (256, 128), 0).astype(F32)
+        mine = self.me[p].astype(F32)
         for a in range(RING):
             k0 = gath[p, 2 * a, 0:16, :].astype(F32)
             k1 = gath[p, 2 * a + 1, 0:16, :].astype(F32)
             high_key = jnp.where(lane < ITEMS, k0[0:1, :], k1[0:1, :])
             low_key = jnp.where(lane < ITEMS, k0[8:9, :], k1[8:9, :])
             key = jnp.where(high_key == mine, low_key, -1.0)
-            mask[:, a * 128 : (a + 1) * 128] = jnp.where(rows == key, 1.0, 0.0).astype(BF16)
-
-        @pl.loop(0, 8)
-        def _(pair):
-            def level(fl):
-                start = pl.multiple_of(16 + fl * ITEMS, 16)
-                return jnp.concatenate([gath[p, s, pl.ds(start, ITEMS), :] for s in range(8)], axis=0)
-
-            rhs = jnp.concatenate([level(2 * pair), level(2 * pair + 1)], axis=1)
-            out = jnp.dot(mask[...], rhs, preferred_element_type=F32).astype(BF16)
-            for side in range(2):
-                start = pl.multiple_of((2 * pair + side) * 64, 64)
-                for b in range(RING):
-                    part_sum[p, b, pl.ds(start, 64), :] = out[b * 64 : (b + 1) * 64, side * 128 : (side + 1) * 128]
-
-        nxt, prv = moved(at, second, 1), moved(at, second, 3)
-        up, down, far = nxt[second], prv[second], lax.rem(at[second] + 2, RING)
-        copies.start(base + 13, part_sum.at[p, far, h0], relay.at[p, 0], nxt)
-        copies.start(base + 14, part_sum.at[p, far, h1], relay.at[p, 1], prv)
-        copies.start(base + 15, part_sum.at[p, up, h1], ring_in.at[p, 0, h1], nxt)
-        copies.start(base + 16, part_sum.at[p, down, h0], ring_in.at[p, 1, h0], prv)
-
-    for p, (first, second, third) in enumerate(PARTS):
-        base = p * PER_PART
-        nxt, prv = moved(at, second, 1), moved(at, second, 3)
-        for index, side, there, half in ((13, 0, nxt, h0), (14, 1, prv, h1)):
-            copies.arrived(base + index)
-            to = there[second]
-            total = part_sum[p, to, half, :].astype(F32) + relay[p, side].astype(F32)
-            part_sum[p, to, half, :] = total.astype(BF16)
-            copies.start(base + index + 4, part_sum.at[p, to, half], ring_in.at[p, side, half], there)
-
-    for p, (first, second, third) in enumerate(PARTS):
-        base = p * PER_PART
-        copies.arrived(*[base + k for k in (15, 16, 17, 18)])
-        own = at[second]
-
-        @pl.loop(0, 16)
-        def _(fl):
-            start = pl.multiple_of(fl * 64, 64)
-            block = pl.ds(start, 64)
-            total = part_sum[p, own, block, :].astype(F32) + ring_in[p, 0, block, :].astype(F32) + ring_in[p, 1, block, :].astype(F32)
-            full[p, block, :] = total
-            narrow = total.astype(BF16)
-            for c in range(RING):
-                cut_sum[p, c, pl.ds(pl.multiple_of(fl * 16, 16), 16), :] = narrow[c * 16 : (c + 1) * 16, :]
-
+            mask[p, :, a * 128 : (a + 1) * 128] = jnp.where(rows == key, 1.0, 0.0).astype(BF16)
+
+    def add_up(self, p, half):
+        gath, part_sum = self.gath, self.part_sum
+        if half == 0:
+            self.arrived(p, 4, 6, 10, 11)
+            self.build_mask(p)
+        else:
+            self.arrived(p, 8, 9, 12)
+
+        @pl.loop(0, 2)
+        def _(twice):
+            for inner in range(2):
+                pair = half * 4 + twice * 2 + inner
+
+                def level(fl):
+                    start = pl.multiple_of(16 + fl * ITEMS, 16)
+                    return jnp.concatenate([gath[p, s, pl.ds(start, ITEMS), :] for s in range(8)], axis=0)
+
+                rhs = jnp.concatenate([level(2 * pair), level(2 * pair + 1)], axis=1)
+                out = jnp.dot(self.mask[p], rhs, preferred_element_type=F32).astype(BF16)
+                for side in range(2):
+                    start = pl.multiple_of((2 * pair + side) * 64, 64)
+                    for b in range(RING):
+                        part_sum[p, b, pl.ds(start, 64), :] = out[b * 64 : (b + 1) * 64, side * 128 : (side + 1) * 128]
+
+        nxt, prv = self.toward(p, 1, 1), self.toward(p, 1, 3)
+        dim = PARTS[p][1]
+        far, rows = lax.rem(self.at[dim] + 2, RING), self.sum_rows[half]
+        if half == 0:
+            self.send(p, 13, part_sum.at[p, far, rows], self.relay.at[p, 0], nxt)
+            self.send(p, 16, part_sum.at[p, prv[dim], rows], self.ring_in.at[p, 1, rows], prv)
+        else:
+            self.send(p, 14, part_sum.at[p, far, rows], self.relay.at[p, 1], prv)
+            self.send(p, 15, part_sum.at[p, nxt[dim], rows], self.ring_in.at[p, 0, rows], nxt)
+
+    def ring_on(self, p, half):
+        there = self.toward(p, 1, 3 if half else 1)
+        to, rows = there[PARTS[p][1]], self.sum_rows[half]
+        self.arrived(p, 13 + half)
+        total = self.part_sum[p, to, rows, :].astype(F32) + self.relay[p, half].astype(F32)
+        self.part_sum[p, to, rows, :] = total.astype(BF16)
+        self.send(p, 17 + half, self.part_sum.at[p, to, rows], self.ring_in.at[p, half, rows], there)
+
+    def ring_end(self, p, half):
+        part_sum, ring_in, full, cut_sum = self.part_sum, self.ring_in, self.full, self.cut_sum
+        if half == 0:
+            self.arrived(p, 16, 17)
+        else:
+            self.arrived(p, 15, 18)
+        own = self.at[PARTS[p][1]]
+
+        @pl.loop(0, 4)
+        def _(quad):
+            for inner in range(2):
+                fl = half * 8 + quad * 2 + inner
+                block = pl.ds(pl.multiple_of(fl * 64, 64), 64)
+                total = part_sum[p, own, block, :].astype(F32) + ring_in[p, 0, block, :].astype(F32) + ring_in[p, 1, block, :].astype(F32)
+                full[p, block, :] = total
+                narrow = total.astype(BF16)
+                for c in range(RING):
+                    cut_sum[p, c, pl.ds(pl.multiple_of(fl * 16, 16), 16), :] = narrow[c * 16 : (c + 1) * 16, :]
+
+        rows = pl.ds(half * 128, 128)
         for k, by in enumerate((1, 3, 2)):
-            there = moved(at, third, by)
-            copies.start(base + 19 + k, cut_sum.at[p, there[third]], last_in.at[p, k], there)
-
-    for p, (first, second, third) in enumerate(PARTS):
-        base = p * PER_PART
-        copies.arrived(base + 19, base + 20, base + 21)
-        for fl in range(16):
-            start = pl.multiple_of(fl * 64 + at[third] * 16, 16)
+            there = self.toward(p, 2, by)
+            self.send(p, 19 + half * 3 + k, cut_sum.at[p, there[PARTS[p][2]], rows], self.last_in.at[p, k, rows], there)
+
+    def close(self, p, half):
+        self.arrived(p, *[19 + half * 3 + k for k in range(3)])
+        for fl in range(half * 8, half * 8 + 8):
+            start = pl.multiple_of(fl * 64 + self.at[PARTS[p][2]] * 16, 16)
             here = slice(fl * 16, fl * 16 + 16)
-            total = full[p, pl.ds(start, 16), :]
+            total = self.full[p, pl.ds(start, 16), :]
             for k in range(3):
-                total = total + last_in[p, k, here, :].astype(F32)
-            mx_ref[p * 256 + fl * 16 : p * 256 + fl * 16 + 16, :] = total
+                total = total + self.last_in[p, k, here, :].astype(F32)
+            self.mx_ref[p * 256 + fl * 16 : p * 256 + fl * 16 + 16, :] = total
 
 
 def contributions(met_ref, weight_ref, cs):
@@ -195,7 +234,7 @@
 REGRID_SCRATCH = [
     pltpu.VMEM((48 * ITEMS, 128), F32),
     pltpu.VMEM((3, 8, SLAB, 128), BF16),
-    pltpu.VMEM((256, 512), BF16),
+    pltpu.VMEM((3, 256, 512), BF16),
     pltpu.VMEM((3, RING, 1024, 128), BF16),
     pltpu.VMEM((3, 2, 512, 128), BF16),
     pltpu.VMEM((3, 2, 1024, 128), BF16),
@@ -219,7 +258,8 @@
 
 
 SPECIES = 256
-HALO_COPIES = 66
+UNROLL = 4
+HALO_COPIES = 75
 
 
 def lanes_of(shape, dim):
@@ -261,10 +301,9 @@
     return copies
 
 
-def first_halos(near, copies, loads, amount, narrow, pick, edges, row_in, edge_in):
+def first_rows(near, copies, loads, amount, narrow, row_in):
     for copy in loads:
         copy.wait()
-    count = 250
 
     @pl.loop(0, 64)
     def _(lr):
@@ -273,6 +312,8 @@
     copies.start(HALO_COPIES + 0, narrow.at[:, 15], row_in.at[0, 0], near["n"])
     copies.start(HALO_COPIES + 1, narrow.at[:, 0], row_in.at[0, 1], near["s"])
 
+
+def first_columns(near, copies, narrow, pick, edges, edge_in):
     @pl.loop(0, 4)
     def _(l):
         edges[0, l] = picked_edges(narrow, pick, l)
@@ -281,12 +322,14 @@
     copies.start(HALO_COPIES + 3, edges.at[0], edge_in.at[0, 1], near["w"])
 
 
-def coefficients(near, copies, mx_ref, courant, courant_in, shifted, coef, band):
+def send_courant(near, copies, mx_ref, courant, courant_in):
     courant[0] = 0.3 * jnp.tanh(mx_ref[0:64, :])
     courant[1] = 0.3 * jnp.tanh(mx_ref[64:128, :])
     copies.start(HALO_COPIES + 4, courant.at[0], courant_in.at[0], near["n"])
     copies.start(HALO_COPIES + 5, courant.at[1], courant_in.at[1], near["e"])
 
+
+def light_of(mx_ref):
     depth = jnp.zeros((16, 128), F32)
     for l in range(4):
         value = mx_ref[128 + l * 16 : 144 + l * 16, :]
@@ -294,6 +337,8 @@
         mx_ref[768 + l * 16 : 784 + l * 16, :] = jnp.exp(-depth)
     mx_ref[832:1024, :] = jnp.zeros((192, 128), F32)
 
+
+def coefficients(copies, courant, courant_in, shifted, coef, band):
     row, lane = lanes_of((128, 128), 0), lanes_of((128, 128), 1)
     from_west = jnp.where(row == lane - 1, 1.0, 0.0)
     from_east = jnp.where(row == lane + 1, 1.0, 0.0)
@@ -326,38 +371,42 @@
     even = lax.rem(lanes_of((SPECIES, 128), 1), 2) == 0
     side[...] = jnp.where(even, edge_in[step, 0, l].astype(F32), edge_in[step, 1, l].astype(F32)).astype(BF16)
 
-    @pl.loop(0, 16)
-    def _(r):
-        lhs = jnp.concatenate([narrow[l, r], side[...]], axis=1)
-        across = jnp.dot(lhs, band[l, r], preferred_element_type=F32)
-        total = coef[l, 0, pl.ds(r, 1), :] * source[l, r + 1] + coef[l, 1, pl.ds(r, 1), :] * source[l, r]
-        total = total + coef[l, 2, pl.ds(r, 1), :] * source[l, r + 2] + across
-        target[l, r + 1] = total
-        if keep:
-            narrow[l, r] = total.astype(BF16)
-
-
-def advect(near, copies, adv_ref, amount, middle, narrow, side, pick, edges, coef, band, row_in, edge_in, store):
-    copies.arrived(*[HALO_COPIES + k for k in range(4)])
-    copies.sent_of(HALO_COPIES + 0, HALO_COPIES + 1)
-    for l in range(4):
-        advance(amount, middle, narrow, side, coef, band, row_in, edge_in, 0, l, True)
-        base = HALO_COPIES + 6 + 4 * l
-        copies.start(base + 0, narrow.at[l, 15], row_in.at[1, 0, l], near["n"])
-        copies.start(base + 1, narrow.at[l, 0], row_in.at[1, 1, l], near["s"])
-        edges[1, l] = picked_edges(narrow, pick, l)
-        copies.start(base + 2, edges.at[1, l], edge_in.at[1, 0, l], near["e"])
-        copies.start(base + 3, edges.at[1, l], edge_in.at[1, 1, l], near["w"])
-    stores = []
-    for l in range(4):
-        base = HALO_COPIES + 6 + 4 * l
-        copies.arrived(*[base + k for k in range(4)])
-        advance(middle, amount, narrow, side, coef, band, row_in, edge_in, 1, l, False)
-        copy = pltpu.make_async_copy(amount.at[l, pl.ds(1, 16)], adv_ref.at[l], store.at[l])
-        copy.start()
-        stores.append(copy)
-    for copy in stores:
-        copy.wait()
+    @pl.loop(0, 16 // UNROLL)
+    def _(group):
+        across = []
+        for k in range(UNROLL):
+            r = group * UNROLL + k
+            lhs = jnp.concatenate([narrow[l, r], side[...]], axis=1)
+            across.append(jnp.dot(lhs, band[l, r], preferred_element_type=F32))
+        for k in range(UNROLL):
+            r = group * UNROLL + k
+            total = coef[l, 0, pl.ds(r, 1), :] * source[l, r + 1] + coef[l, 1, pl.ds(r, 1), :] * source[l, r]
+            total = total + coef[l, 2, pl.ds(r, 1), :] * source[l, r + 2] + across[k]
+            target[l, r + 1] = total
+            if keep:
+                narrow[l, r] = total.astype(BF16)
+
+
+def first_step(near, copies, l, amount, middle, narrow, side, pick, edges, coef, band, row_in, edge_in):
+    if l == 0:
+        copies.arrived(*[HALO_COPIES + k for k in range(4)])
+        copies.sent_of(HALO_COPIES + 0, HALO_COPIES + 1)
+    advance(amount, middle, narrow, side, coef, band, row_in, edge_in, 0, l, True)
+    base = HALO_COPIES + 6 + 4 * l
+    copies.start(base + 0, narrow.at[l, 15], row_in.at[1, 0, l], near["n"])
+    copies.start(base + 1, narrow.at[l, 0], row_in.at[1, 1, l], near["s"])
+    edges[1, l] = picked_edges(narrow, pick, l)
+    copies.start(base + 2, edges.at[1, l], edge_in.at[1, 0, l], near["e"])
+    copies.start(base + 3, edges.at[1, l], edge_in.at[1, 1, l], near["w"])
+
+
+def second_step(copies, l, adv_ref, amount, middle, narrow, side, coef, band, row_in, edge_in, store):
+    base = HALO_COPIES + 6 + 4 * l
+    copies.arrived(*[base + k for k in range(4)])
+    advance(middle, amount, narrow, side, coef, band, row_in, edge_in, 1, l, False)
+    copy = pltpu.make_async_copy(amount.at[l, pl.ds(1, 16)], adv_ref.at[l], store.at[l])
+    copy.start()
+    return copy
 
 
 ADVECT_SCRATCH = [
@@ -389,18 +438,59 @@
     pl.semaphore_wait(barrier, count)
     copies = Copies(send, recv)
 
-    def meanwhile():
-        edge_picker(pick)
-
-        @pl.loop(0, 64)
-        def _(k):
-            band[k // 16, lax.rem(k, 16), 128:256, :] = jnp.zeros((128, 128), BF16)
-
-        first_halos(near, copies, loads, amount, narrow, pick, edges, row_in, edge_in)
-
-    regrid(at, copies, met_ref, weight_ref, key_ref, mx_ref, *regrid_scratch, meanwhile=meanwhile)
-    coefficients(near, copies, mx_ref, courant, courant_in, shifted, coef, band)
-    advect(near, copies, adv_ref, amount, middle, narrow, side, pick, edges, coef, band, row_in, edge_in, store)
+    flow = Regrid(at, copies, key_ref, mx_ref, *regrid_scratch)
+    every = range(3)
+    for p in every:
+        flow.open(p)
+
+    edge_picker(pick)
+
+    @pl.loop(0, 64)
+    def _(k):
+        band[k // 16, lax.rem(k, 16), 128:256, :] = jnp.zeros((128, 128), BF16)
+
+    for p in every:
+        flow.low_first(p)
+        flow.low_second(p)
+    first_rows(near, copies, loads, amount, narrow, row_in)
+    for p in every:
+        flow.high_first(p)
+    first_columns(near, copies, narrow, pick, edges, edge_in)
+    for p in every:
+        flow.low_third(p)
+    for p in every:
+        flow.add_up(p, 0)
+    for p in every:
+        flow.high_rest(p)
+    for p in every:
+        flow.ring_on(p, 0)
+    flow.add_up(0, 1)
+    flow.ring_end(0, 0)
+    flow.add_up(1, 1)
+    flow.add_up(2, 1)
+    for p in every:
+        flow.ring_on(p, 1)
+    flow.close(0, 0)
+    send_courant(near, copies, mx_ref, courant, courant_in)
+    flow.ring_end(1, 0)
+    flow.ring_end(2, 0)
+    coefficients(copies, courant, courant_in, shifted, coef, band)
+    first = (amount, middle, narrow, side, pick, edges, coef, band, row_in, edge_in)
+    second = (adv_ref, amount, middle, narrow, side, coef, band, row_in, edge_in, store)
+    flow.ring_end(0, 1)
+    first_step(near, copies, 0, *first)
+    flow.ring_end(1, 1)
+    flow.ring_end(2, 1)
+    for l in range(1, 4):
+        first_step(near, copies, l, *first)
+    stores = [second_step(copies, l, *second) for l in range(4)]
+    flow.close(0, 1)
+    light_of(mx_ref)
+    for p in (1, 2):
+        for half in range(2):
+            flow.close(p, half)
+    for copy in stores:
+        copy.wait()
     copies.sent()
 
 
@@ -451,7 +541,7 @@
             lr = k * CHUNK + 2 * pair
             rhs = jnp.concatenate([fields(lr), fields(lr + 1)], axis=1)
             exponent = jnp.dot(rate_ref[...], rhs, preferred_element_type=F32)
-            loss = jnp.maximum(exponent, 0.0) + jnp.log1p(jnp.exp(-jnp.abs(exponent)))
+            loss = jnp.maximum(exponent, 0.0) + jnp.log(1.0 + jnp.exp(-jnp.abs(exponent)))
             for side in range(2):
                 result[lr + side] = amount[lr + side] / (1.0 + loss[:, side * 128 : side * 128 + 128])
                 put(lr + side).start()
@@ -470,7 +560,7 @@
         in_specs=[vmem, vmem, anywhere],
         out_specs=(vmem, anywhere),
         scratch_shapes=[pltpu.VMEM((64, SPECIES, 128), F32), pltpu.VMEM((64, SPECIES, 128), F32), dma((64 // CHUNK,)), dma((64,))],
-        compiler_params=pltpu.CompilerParams(vmem_limit_bytes=40 << 20),
+        compiler_params=pltpu.CompilerParams(vmem_limit_bytes=62 << 20),
         name="chemistry",
     )(mx, rates, adv)
 

time: 98.1 us -> 76.4 us (0.78)
  Pallas kernels: 89.9 us -> 71.8 us
  local copies, waits for them, and re-layouts: 4.73 us -> 0.94 us
    pallas_call x1, Pallas kernels: 79 us -> 61 us  [transport_call(): pl.pallas_call(transport_kernel, out_shape=(jax.ShapeDtypeStruct((1024, 1...]
    unnamed x4 -> x0, local copies, waits for them, and re-layouts: 4.42 us -> none
where the time goes in v3:
time: 76.4 us; the launch traced here: 75.8 us
  Pallas kernels  71.8 us (94%)
  other arithmetic  2.33 us (3%)
  local copies, waits for them, and re-layouts  0.94 us (1%)
    pallas_call x1, Pallas kernels, transport_call(): pl.pallas_call(transport_kernel, out_shape=(jax.ShapeDtypeStruct((1024, 1...  61 us
    pallas_call x1, Pallas kernels, chemistry_call(): pl.pallas_call(chemistry_kernel, out_shape=(jax.ShapeDtypeStruct((768, 12...  10.9 us

profile of v3, /device:TPU:0, one launch (start us, length us, event | category | flops | bytes accessed | tf_op | source)
XLA Modules:
  0.0 75.8 jit_solution(17701079016456253699)
XLA Ops:
  0.6 0.7 add_bitcast_fusion.4
  1.4 0.1 maximum_bitcast_fusion.2
  1.4 0.1 maximum_bitcast_fusion
  1.5 0.1 maximum_bitcast_fusion.1
  1.6 0.6 pad_maximum_fusion.1.key_ref
  2.2 0.7 pad_maximum_fusion
  3.0 0.1 copy.13
  3.1 0.8 %concatenate.23.rate_ref = bf16[256,96]{1,0:T(8,128)(2,1)} concatenate(bf16[256,16]{1,0:T(8,128)(2,1)S(1)} %get-tuple-element.12, bf16[256,16]{1,0:T(8,128)(2,1)S(1)} %get-tuple-element.12, bf16[256,16]{1,0:T(8,128)(2,1)S(1)} %get-tuple-element.12, bf16[256,16]{1,0:T(8,128)(2,1)S(1)} %get-tuple-element.11, bf16[256,16]{1,0:T(8,128)(2,1)S(1)} %get-tuple-element.11, ...), dimensions={1} | concatenate | bytes 98304 | tf_op jit(solution)/shard_map/concatenate | solution.py:574
  3.9 61.0 %transport.1 = (f32[1024,128]{1,0:T(8,128)}, f32[4,16,256,128]{3,2,1,0:T(8,128)}) custom-call(bf16[64,48,128]{2,1,0:T(8,128)(2,1)} %met_ref.1, bf16[64,128,128]{2,1,0:T(8,128)(2,1)} %weight_ref.1, bf16[3,16,128]{2,1,0:T(8,128)(2,1)} %pad_maximum_fusion.1.key_ref, f32[250,64,1,128]{3,2,1,0:T(1,128)} %bitcast.30), custom_call_target="tpu_custom_call" | custom-call | tf_op jit(solution)/shard_map/transport/pallas_call | solution.py:500
  64.9 10.9 %chemistry.1 = (f32[768,128]{1,0:T(8,128)}, f32[250,64,1,128]{3,2,1,0:T(1,128)}) custom-call(f32[1024,128]{1,0:T(8,128)} %get-tuple-element.6.mx_ref, bf16[256,96]{1,0:T(8,128)(2,1)} %concatenate.23.rate_ref, f32[64,256,128]{2,1,0:T(8,128)} %bitcast.29), custom_call_target="tpu_custom_call" | custom-call | tf_op jit(solution)/shard_map/chemistry/pallas_call | solution.py:557
  (6 shorter events, 0.1 us)

commit v4 on v3

--- a/solution.py
+++ b/solution.py
@@ -214,11 +214,11 @@
             self.mx_ref[p * 256 + fl * 16 : p * 256 + fl * 16 + 16, :] = total
 
 
-def contributions(met_ref, weight_ref, cs):
-    @pl.loop(0, ITEMS // 4)
+def contributions(met_ref, weight_ref, cs, part):
+    @pl.loop(0, ITEMS // 16)
     def _(group):
         for k in range(4):
-            s = group * 4 + k
+            s = part * (ITEMS // 4) + group * 4 + k
             cs[pl.ds(s, 48, stride=ITEMS), :] = jnp.dot(met_ref[s], weight_ref[s], preferred_element_type=F32)
 
 
@@ -244,17 +244,17 @@
 ]
 
 
-def keys_of(block_dest, block_row):
-    face, tile = block_dest >> 4, block_dest & 15
+def keys_of(dest, row):
+    dest, row = jnp.concatenate([dest, dest], axis=1), jnp.concatenate([row, row], axis=1)
+    face, tile = dest >> 4, dest & 15
     pos = {"x": tile & 3, "y": face >> 1, "z": tile >> 2}
+    upper = lax.broadcasted_iota(jnp.int32, (16, 128), 0) < 8
     out = []
     for first, second, third in PARTS:
         high = pos[first] * 2 + (face & 1)
-        low = pos[second] * 64 + pos[third] * 16 + block_row
-        both = jnp.stack([high, low])[:, None, :]
-        both = jnp.broadcast_to(both, (2, 8, ITEMS)).reshape(16, ITEMS)
-        out.append(jnp.concatenate([both, both], axis=1))
-    return jnp.stack(out).astype(BF16)
+        low = pos[second] * 64 + pos[third] * 16 + row
+        out.append(jnp.where(upper, high.astype(F32), low.astype(F32)).astype(BF16))
+    return out
 
 
 SPECIES = 256
@@ -268,15 +268,18 @@
 
 def edge_picker(pick):
     row, lane = lanes_of((128, 128), 0), lanes_of((128, 128), 1)
-    for r in range(16):
-        east = jnp.logical_and(row == 127, lane == 2 * r)
-        west = jnp.logical_and(row == 0, lane == 2 * r + 1)
-        pick[r * 128 : (r + 1) * 128, :] = jnp.where(jnp.logical_or(east, west), 1.0, 0.0).astype(BF16)
+
+    @pl.loop(0, 64)
+    def _(lr):
+        east = jnp.logical_and(row == 127, lane == 2 * lr)
+        west = jnp.logical_and(row == 0, lane == 2 * lr + 1)
+        pick[pl.ds(pl.multiple_of(lr * 128, 128), 128), :] = jnp.where(jnp.logical_or(east, west), 1.0, 0.0).astype(BF16)
 
 
 def picked_edges(narrow, pick, l):
     rows = jnp.concatenate([narrow[l, r] for r in range(16)], axis=1)
-    return jnp.dot(rows, pick[...], preferred_element_type=F32).astype(BF16)
+    start = l * 2048 if isinstance(l, int) else pl.multiple_of(l * 2048, 2048)
+    return jnp.dot(rows, pick[pl.ds(start, 2048), :], preferred_element_type=F32)
 
 
 def neighbours():
@@ -309,15 +312,14 @@
     def _(lr):
         narrow[lr // 16, lax.rem(lr, 16)] = amount[lr // 16, lax.rem(lr, 16) + 1].astype(BF16)
 
+
+def first_columns(near, copies, narrow, pick, edges, edge_in):
+    edges[0] = lax.fori_loop(0, 4, lambda l, total: total + picked_edges(narrow, pick, l), jnp.zeros((SPECIES, 128), F32)).astype(BF16)
+
+
+def first_sends(near, copies, narrow, edges, row_in, edge_in):
     copies.start(HALO_COPIES + 0, narrow.at[:, 15], row_in.at[0, 0], near["n"])
     copies.start(HALO_COPIES + 1, narrow.at[:, 0], row_in.at[0, 1], near["s"])
-
-
-def first_columns(near, copies, narrow, pick, edges, edge_in):
-    @pl.loop(0, 4)
-    def _(l):
-        edges[0, l] = picked_edges(narrow, pick, l)
-
     copies.start(HALO_COPIES + 2, edges.at[0], edge_in.at[0, 0], near["e"])
     copies.start(HALO_COPIES + 3, edges.at[0], edge_in.at[0, 1], near["w"])
 
@@ -358,18 +360,19 @@
         for r in range(16):
             w, e = west[r : r + 1, :], east[r : r + 1, :]
             band[l, r, 0:128, :] = (from_west * w + from_east * e).astype(BF16)
-            k = 2 * r % 16
+            lr = l * 16 + r
+            k = 2 * lr % 16
             ends = jnp.where(jnp.logical_and(sub == k, edge == 0), w, jnp.where(jnp.logical_and(sub == k + 1, edge == 127), e, 0.0))
-            other = 128 + 16 * (1 - r // 8)
-            band[l, r, 128 + 16 * (r // 8) : 144 + 16 * (r // 8), :] = ends.astype(BF16)
-            band[l, r, other : other + 16, :] = jnp.zeros((16, 128), BF16)
+            band[l, r, 128 + 16 * (lr // 8) : 144 + 16 * (lr // 8), :] = ends.astype(BF16)
 
 
 def advance(source, target, narrow, side, coef, band, row_in, edge_in, step, l, keep):
     source[l, 0] = row_in[step, 0, l].astype(F32)
     source[l, 17] = row_in[step, 1, l].astype(F32)
     even = lax.rem(lanes_of((SPECIES, 128), 1), 2) == 0
-    side[...] = jnp.where(even, edge_in[step, 0, l].astype(F32), edge_in[step, 1, l].astype(F32)).astype(BF16)
+    if step == 0 and l == 0 or step == 1 and l % 2 == 0:
+        slot = 0 if step == 0 else 1 + l // 2
+        side[...] = jnp.where(even, edge_in[slot, 0].astype(F32), edge_in[slot, 1].astype(F32)).astype(BF16)
 
     @pl.loop(0, 16 // UNROLL)
     def _(group):
@@ -382,7 +385,7 @@
             r = group * UNROLL + k
             total = coef[l, 0, pl.ds(r, 1), :] * source[l, r + 1] + coef[l, 1, pl.ds(r, 1), :] * source[l, r]
             total = total + coef[l, 2, pl.ds(r, 1), :] * source[l, r + 2] + across[k]
-            target[l, r + 1] = total
+            target[l, r + keep] = total
             if keep:
                 narrow[l, r] = total.astype(BF16)
 
@@ -395,18 +398,19 @@
     base = HALO_COPIES + 6 + 4 * l
     copies.start(base + 0, narrow.at[l, 15], row_in.at[1, 0, l], near["n"])
     copies.start(base + 1, narrow.at[l, 0], row_in.at[1, 1, l], near["s"])
-    edges[1, l] = picked_edges(narrow, pick, l)
-    copies.start(base + 2, edges.at[1, l], edge_in.at[1, 0, l], near["e"])
-    copies.start(base + 3, edges.at[1, l], edge_in.at[1, 1, l], near["w"])
-
-
-def second_step(copies, l, adv_ref, amount, middle, narrow, side, coef, band, row_in, edge_in, store):
+    if l % 2 == 1:
+        slot = 1 + l // 2
+        edges[slot] = (picked_edges(narrow, pick, l - 1) + picked_edges(narrow, pick, l)).astype(BF16)
+        copies.start(base + 2, edges.at[slot], edge_in.at[slot, 0], near["e"])
+        copies.start(base + 3, edges.at[slot], edge_in.at[slot, 1], near["w"])
+
+
+def second_step(copies, l, adv_ref, amount, middle, narrow, side, coef, band, row_in, edge_in):
     base = HALO_COPIES + 6 + 4 * l
-    copies.arrived(*[base + k for k in range(4)])
-    advance(middle, amount, narrow, side, coef, band, row_in, edge_in, 1, l, False)
-    copy = pltpu.make_async_copy(amount.at[l, pl.ds(1, 16)], adv_ref.at[l], store.at[l])
-    copy.start()
-    return copy
+    copies.arrived(base + 0, base + 1)
+    if l % 2 == 0:
+        copies.arrived(base + 6, base + 7)
+    advance(middle, adv_ref, narrow, side, coef, band, row_in, edge_in, 1, l, False)
 
 
 ADVECT_SCRATCH = [
@@ -414,10 +418,10 @@
     pltpu.VMEM((4, 18, SPECIES, 128), F32),
     pltpu.VMEM((4, 16, SPECIES, 128), BF16),
     pltpu.VMEM((SPECIES, 128), BF16),
-    pltpu.VMEM((2048, 128), BF16),
-    pltpu.VMEM((2, 4, SPECIES, 128), BF16),
+    pltpu.VMEM((8192, 128), BF16),
+    pltpu.VMEM((3, SPECIES, 128), BF16),
     pltpu.VMEM((2, 2, 4, SPECIES, 128), BF16),
-    pltpu.VMEM((2, 2, 4, SPECIES, 128), BF16),
+    pltpu.VMEM((3, 2, SPECIES, 128), BF16),
     pltpu.VMEM((2, 64, 128), F32),
     pltpu.VMEM((2, 64, 128), F32),
     pltpu.VMEM((4, 24, 128), F32),
@@ -427,18 +431,30 @@
 COPIES = HALO_COPIES + 22
 
 
-def transport_kernel(met_ref, weight_ref, key_ref, tracer_ref, mx_ref, adv_ref, send, recv, load, store, *scratch):
+def transport_kernel(met_hbm, weight_hbm, dest_ref, row_ref, tracer_ref, mx_ref, adv_ref, send, recv, load, fetch, met_ref, weight_ref, *scratch):
     cut = len(REGRID_SCRATCH)
     regrid_scratch = scratch[:cut]
     amount, middle, narrow, side, pick, edges, row_in, edge_in, courant, courant_in, shifted, coef, band = scratch[cut:]
     at, near = whereabouts(), neighbours()
+    quarter = ITEMS // 4
+    blocks = []
+    for k in range(4):
+        some = pl.ds(k * quarter, quarter)
+        for which, (src, dst) in enumerate(((weight_hbm, weight_ref), (met_hbm, met_ref))):
+            copy = pltpu.make_async_copy(src.at[some], dst.at[some], fetch.at[2 * k + which])
+            copy.start()
+            blocks.append(copy)
+    barrier, count = greet(at, near)
     loads = start_tracers(tracer_ref, amount, load)
-    barrier, count = greet(at, near)
-    contributions(met_ref, weight_ref, regrid_scratch[0])
+    for k in range(4):
+        blocks[2 * k].wait()
+        blocks[2 * k + 1].wait()
+        contributions(met_ref, weight_ref, regrid_scratch[0], k)
+    keys = keys_of(dest_ref[...], row_ref[...])
     pl.semaphore_wait(barrier, count)
     copies = Copies(send, recv)
 
-    flow = Regrid(at, copies, key_ref, mx_ref, *regrid_scratch)
+    flow = Regrid(at, copies, keys, mx_ref, *regrid_scratch)
     every = range(3)
     for p in every:
         flow.open(p)
@@ -452,9 +468,9 @@
     for p in every:
         flow.low_first(p)
         flow.low_second(p)
+    for p in every:
+        flow.high_first(p)
     first_rows(near, copies, loads, amount, narrow, row_in)
-    for p in every:
-        flow.high_first(p)
     first_columns(near, copies, narrow, pick, edges, edge_in)
     for p in every:
         flow.low_third(p)
@@ -464,6 +480,7 @@
         flow.high_rest(p)
     for p in every:
         flow.ring_on(p, 0)
+    first_sends(near, copies, narrow, edges, row_in, edge_in)
     flow.add_up(0, 1)
     flow.ring_end(0, 0)
     flow.add_up(1, 1)
@@ -476,55 +493,69 @@
     flow.ring_end(2, 0)
     coefficients(copies, courant, courant_in, shifted, coef, band)
     first = (amount, middle, narrow, side, pick, edges, coef, band, row_in, edge_in)
-    second = (adv_ref, amount, middle, narrow, side, coef, band, row_in, edge_in, store)
+    second = (adv_ref, amount, middle, narrow, side, coef, band, row_in, edge_in)
     flow.ring_end(0, 1)
     first_step(near, copies, 0, *first)
     flow.ring_end(1, 1)
     flow.ring_end(2, 1)
     for l in range(1, 4):
         first_step(near, copies, l, *first)
-    stores = [second_step(copies, l, *second) for l in range(4)]
+    for l in range(4):
+        second_step(copies, l, *second)
     flow.close(0, 1)
     light_of(mx_ref)
     for p in (1, 2):
         for half in range(2):
             flow.close(p, half)
-    for copy in stores:
-        copy.wait()
     copies.sent()
 
 
-def transport_call(met_src, weights, keys, tracers):
+def transport_call(met_src, weights, dest, row, tracers):
     vmem, anywhere = pl.BlockSpec(memory_space=pltpu.VMEM), pl.BlockSpec(memory_space=pl.ANY)
     dma = pltpu.SemaphoreType.DMA
     return pl.pallas_call(
         transport_kernel,
-        out_shape=(jax.ShapeDtypeStruct((1024, 128), F32), jax.ShapeDtypeStruct((4, 16, SPECIES, 128), F32)),
-        in_specs=[vmem] * 3 + [anywhere],
-        out_specs=(vmem, anywhere),
-        scratch_shapes=[dma((COPIES,)), dma((COPIES,)), dma((64,)), dma((4,))] + REGRID_SCRATCH + ADVECT_SCRATCH,
-        compiler_params=pltpu.CompilerParams(collective_id=0, has_side_effects=True, vmem_limit_bytes=60 << 20),
+        out_shape=(pltpu.VMEM((1024, 128), F32), pltpu.VMEM((4, 16, SPECIES, 128), F32)),
+        in_specs=[anywhere, anywhere, vmem, vmem, anywhere],
+        out_specs=(vmem, vmem),
+        scratch_shapes=[dma((COPIES,)), dma((COPIES,)), dma((64,)), dma((8,)), pltpu.VMEM(met_src.shape, BF16), pltpu.VMEM(weights.shape, BF16)] + REGRID_SCRATCH + ADVECT_SCRATCH,
+        compiler_params=pltpu.CompilerParams(collective_id=0, has_side_effects=True, vmem_limit_bytes=54 << 20),
         name="transport",
-    )(met_src, weights, keys, tracers)
+    )(met_src, weights, dest, row, tracers)
 
 
 CHUNK = 4
 
 
-def chemistry_kernel(mx_ref, rate_ref, adv_ref, met_ref, out_ref, amount, result, load, store):
+def thirds(value):
+    first = value.astype(BF16)
+    rest = value - first.astype(F32)
+    second = rest.astype(BF16)
+    return first, second, (rest - second.astype(F32)).astype(BF16)
+
+
+def spread_rates(rate_in, photo_in, both, rates):
+    nfields, count = rate_in.shape
+    both[...] = jnp.zeros(both.shape, F32)
+    both[0:nfields, 0:count] = rate_in[...]
+    both[nfields : nfields + 1, 0:count] = photo_in[...]
+    field, lane = lanes_of((16, 96), 0), lanes_of((16, 96), 1)
+    total = jnp.zeros((SPECIES, 96), F32)
+    for piece, (low, high) in zip(thirds(both[...].T), ((0, 48), (48, 80), (80, 96))):
+        here = jnp.logical_and(jnp.logical_and(lane >= low, lane < high), lax.rem(lane, 16) == field)
+        total = total + jnp.dot(piece, jnp.where(here, 1.0, 0.0).astype(BF16), preferred_element_type=F32)
+    rates[...] = total.astype(BF16)
+
+
+def chemistry_kernel(mx_ref, rate_in, photo_in, adv_ref, met_ref, out_ref, both, rates, result, store):
     chunks = 64 // CHUNK
     count = out_ref.shape[0]
 
-    def fetch(k):
-        rows = pl.ds(k * CHUNK, CHUNK)
-        return pltpu.make_async_copy(adv_ref.at[rows], amount.at[rows], load.at[k])
-
     def put(lr):
         return pltpu.make_async_copy(result.at[lr, pl.ds(0, count)], out_ref.at[:, lr, 0], store.at[lr])
 
-    for k in range(chunks):
-        fetch(k).start()
     met_ref[...] = mx_ref[0:768, :]
+    spread_rates(rate_in, photo_in, both, rates)
 
     def fields(lr):
         value = mx_ref[pl.ds(lr, 16, stride=64), :]
@@ -536,14 +567,13 @@
 
     @pl.loop(0, chunks)
     def _(k):
-        fetch(k).wait()
         for pair in range(CHUNK // 2):
             lr = k * CHUNK + 2 * pair
             rhs = jnp.concatenate([fields(lr), fields(lr + 1)], axis=1)
-            exponent = jnp.dot(rate_ref[...], rhs, preferred_element_type=F32)
+            exponent = jnp.dot(rates[...], rhs, preferred_element_type=F32)
             loss = jnp.maximum(exponent, 0.0) + jnp.log(1.0 + jnp.exp(-jnp.abs(exponent)))
             for side in range(2):
-                result[lr + side] = amount[lr + side] / (1.0 + loss[:, side * 128 : side * 128 + 128])
+                result[lr + side] = adv_ref[lr + side] / (1.0 + loss[:, side * 128 : side * 128 + 128])
                 put(lr + side).start()
 
     @pl.loop(0, 64)
@@ -551,35 +581,24 @@
         put(lr).wait()
 
 
-def chemistry_call(mx, rates, adv, count):
+def chemistry_call(mx, rate_coef, photo_coef, adv, count):
     vmem, anywhere = pl.BlockSpec(memory_space=pltpu.VMEM), pl.BlockSpec(memory_space=pl.ANY)
     dma = pltpu.SemaphoreType.DMA
     return pl.pallas_call(
         chemistry_kernel,
         out_shape=(jax.ShapeDtypeStruct((768, 128), F32), jax.ShapeDtypeStruct((count, 64, 1, 128), F32)),
-        in_specs=[vmem, vmem, anywhere],
+        in_specs=[vmem] * 4,
         out_specs=(vmem, anywhere),
-        scratch_shapes=[pltpu.VMEM((64, SPECIES, 128), F32), pltpu.VMEM((64, SPECIES, 128), F32), dma((64 // CHUNK,)), dma((64,))],
-        compiler_params=pltpu.CompilerParams(vmem_limit_bytes=62 << 20),
+        scratch_shapes=[pltpu.VMEM((16, SPECIES), F32), pltpu.VMEM((SPECIES, 96), BF16), pltpu.VMEM((64, SPECIES, 128), F32), dma((64,))],
+        compiler_params=pltpu.CompilerParams(vmem_limit_bytes=40 << 20),
         name="chemistry",
-    )(mx, rates, adv)
-
-
-def rates_of(rate_coef, photo_coef):
-    both = jnp.concatenate([rate_coef, photo_coef[:, None]], axis=1)
-    both = jnp.pad(both, ((0, SPECIES - both.shape[0]), (0, 16 - both.shape[1])))
-    r1 = lax.reduce_precision(both, 8, 7)
-    r2 = lax.reduce_precision(both - r1, 8, 7)
-    r3 = both - r1 - r2
-    return jnp.concatenate([r1, r1, r1, r2, r2, r3], axis=1).astype(BF16)
+    )(mx, rate_coef, photo_coef, adv)
 
 
 def local(met_src, intersection_weights, block_dest, block_row, tracers, rate_coef, photo_coef):
     species, levels, rows, cells = tracers.shape
-    keys = keys_of(block_dest, block_row)
-    rates = rates_of(rate_coef, photo_coef)
-    mx, adv = transport_call(met_src, intersection_weights, keys, tracers.reshape(species, levels * rows, 1, cells))
-    met, out = chemistry_call(mx, rates, adv.reshape(levels * rows, SPECIES, cells), species)
+    mx, adv = transport_call(met_src, intersection_weights, block_dest[None], block_row[None], tracers.reshape(species, levels * rows, 1, cells))
+    met, out = chemistry_call(mx, rate_coef.T, photo_coef[None], adv.reshape(levels * rows, SPECIES, cells), species)
     return met.reshape(-1, levels, rows, cells), out.reshape(species, levels, rows, cells)
 
 

time: 76.4 us -> 68.5 us (0.90)
  Pallas kernels: 71.8 us -> 67.7 us
  other arithmetic: 2.33 us -> 0 us
  local copies, waits for them, and re-layouts: 0.94 us -> 0.01 us
    pallas_call x1, Pallas kernels: 61 us -> 58.8 us  [transport_call(): pl.pallas_call(transport_kernel, out_shape=(pltpu.VMEM((1024, 128), F32),...]
    pallas_call x1, Pallas kernels: 10.9 us -> 8.92 us  [chemistry_call(): pl.pallas_call(chemistry_kernel, out_shape=(jax.ShapeDtypeStruct((768, 12...]
    another operation x8 -> x0, other arithmetic: 1.59 us -> none  [the longest x4 0.84 us: keys_of(): return jnp.stack(out).astype(BF16)]
    concatenate x2 -> x0, local copies, waits for them, and re-layouts: 0.93 us -> none  [the longest x1 0.81 us: rates_of(): return jnp.concatenate([r1, r1, r1, r2, r2, r3], axis=1).astype(BF16)]
where the time goes in v4:
time: 68.5 us; the launch traced here: 68.4 us
  Pallas kernels  67.7 us (99%)
    pallas_call x1, Pallas kernels, transport_call(): pl.pallas_call(transport_kernel, out_shape=(pltpu.VMEM((1024, 128), F32),...  58.8 us
    pallas_call x1, Pallas kernels, chemistry_call(): pl.pallas_call(chemistry_kernel, out_shape=(jax.ShapeDtypeStruct((768, 12...  8.92 us

profile of v4, /device:TPU:0, one launch (start us, length us, event | category | flops | bytes accessed | tf_op | source)
XLA Modules:
  0.0 68.4 jit_solution(13058740634273398901)
XLA Ops:
  0.6 0.0 copy-start.1
  0.6 0.0 copy-start
  0.7 58.8 %transport.1 = (f32[1024,128]{1,0:T(8,128)S(1)}, f32[4,16,256,128]{3,2,1,0:T(8,128)S(1)}) custom-call(bf16[64,48,128]{2,1,0:T(8,128)(2,1)} %met_hbm.1, bf16[64,128,128]{2,1,0:T(8,128)(2,1)} %weight_hbm.1, s32[1,64]{1,0:T(1,128)} %bitcast.12, s32[1,64]{1,0:T(1,128)} %bitcast.13, f32[250,64,1,128]{3,2,1,0:T(1,128)} %bitcast.11), custom_call_target="tpu_custom_call" | custom-call | tf_op jit(solution)/shard_map/transport/pallas_call | solution.py:516
  59.4 0.0 copy-done.1
  59.4 0.0 copy-done
  59.4 8.9 %chemistry.1 = (f32[768,128]{1,0:T(8,128)}, f32[250,64,1,128]{3,2,1,0:T(1,128)}) custom-call(f32[1024,128]{1,0:T(8,128)S(1)} %get-tuple-element.6.mx_ref, f32[12,250]{1,0:T(8,128)S(1)} %bitcast.9, f32[1,250]{1,0:T(1,128)S(1)} %bitcast.10, f32[64,256,128]{2,1,0:T(8,128)S(1)} %bitcast.8), custom_call_target="tpu_custom_call" | custom-call | tf_op jit(solution)/shard_map/chemistry/pallas_call | solution.py:587
Async XLA Ops:
  0.6 58.8 %copy-start.1 = (f32[250]{0:T(256)S(1)}, f32[250]{0:T(256)}, u32[]{:S(2)}) copy-start(f32[250]{0:T(256)} %param.13) | copy-start | bytes 3004
  0.6 58.8 %copy-start = (f32[250,12]{0,1:T(8,128)S(1)}, f32[250,12]{0,1:T(8,128)}, u32[]{:S(2)}) copy-start(f32[250,12]{0,1:T(8,128)} %param.12) | copy-start | bytes 36004

commit v5 on v4

--- a/solution.py
+++ b/solution.py
@@ -258,7 +258,7 @@
 
 
 SPECIES = 256
-UNROLL = 4
+UNROLL = 8
 HALO_COPIES = 75
 
 
@@ -445,7 +445,6 @@
             copy.start()
             blocks.append(copy)
     barrier, count = greet(at, near)
-    loads = start_tracers(tracer_ref, amount, load)
     for k in range(4):
         blocks[2 * k].wait()
         blocks[2 * k + 1].wait()
@@ -458,6 +457,7 @@
     every = range(3)
     for p in every:
         flow.open(p)
+    loads = start_tracers(tracer_ref, amount, load)
 
     edge_picker(pick)
 
@@ -478,13 +478,13 @@
         flow.add_up(p, 0)
     for p in every:
         flow.high_rest(p)
+    flow.add_up(0, 1)
     for p in every:
         flow.ring_on(p, 0)
-    first_sends(near, copies, narrow, edges, row_in, edge_in)
-    flow.add_up(0, 1)
-    flow.ring_end(0, 0)
     flow.add_up(1, 1)
     flow.add_up(2, 1)
+    flow.ring_end(0, 0)
+    first_sends(near, copies, narrow, edges, row_in, edge_in)
     for p in every:
         flow.ring_on(p, 1)
     flow.close(0, 0)
@@ -524,7 +524,7 @@
     )(met_src, weights, dest, row, tracers)
 
 
-CHUNK = 4
+CHUNK = 16
 
 
 def thirds(value):

time: 68.5 us -> 64.3 us (0.939)
  Pallas kernels: 67.7 us -> 63.1 us
    pallas_call x1, Pallas kernels: 58.8 us -> 56.2 us  [transport_call(): pl.pallas_call(transport_kernel, out_shape=(pltpu.VMEM((1024, 128), F32),...]
    pallas_call x1, Pallas kernels: 8.92 us -> 6.9 us  [chemistry_call(): pl.pallas_call(chemistry_kernel, out_shape=(jax.ShapeDtypeStruct((768, 12...]
where the time goes in v5:
time: 64.3 us; the launch traced here: 63.8 us
  Pallas kernels  63.1 us (98%)
  between operations  0.67 us (1%)
    pallas_call x1, Pallas kernels, transport_call(): pl.pallas_call(transport_kernel, out_shape=(pltpu.VMEM((1024, 128), F32),...  56.2 us
    pallas_call x1, Pallas kernels, chemistry_call(): pl.pallas_call(chemistry_kernel, out_shape=(jax.ShapeDtypeStruct((768, 12...  6.9 us

profile of v5, /device:TPU:0, one launch (start us, length us, event | category | flops | bytes accessed | tf_op | source)
XLA Modules:
  0.0 63.8 jit_solution(14148608038495354129)
XLA Ops:
  0.6 0.0 copy-start.1
  0.6 0.0 copy-start
  0.7 56.2 %transport.1 = (f32[1024,128]{1,0:T(8,128)S(1)}, f32[4,16,256,128]{3,2,1,0:T(8,128)S(1)}) custom-call(bf16[64,48,128]{2,1,0:T(8,128)(2,1)} %met_hbm.1, bf16[64,128,128]{2,1,0:T(8,128)(2,1)} %weight_hbm.1, s32[1,64]{1,0:T(1,128)} %bitcast.12, s32[1,64]{1,0:T(1,128)} %bitcast.13, f32[250,64,1,128]{3,2,1,0:T(1,128)} %bitcast.11), custom_call_target="tpu_custom_call" | custom-call | tf_op jit(solution)/shard_map/transport/pallas_call | solution.py:516
  56.9 0.0 copy-done.1
  56.9 0.0 copy-done
  56.9 6.9 %chemistry.1 = (f32[768,128]{1,0:T(8,128)}, f32[250,64,1,128]{3,2,1,0:T(1,128)}) custom-call(f32[1024,128]{1,0:T(8,128)S(1)} %get-tuple-element.6.mx_ref, f32[12,250]{1,0:T(8,128)S(1)} %bitcast.9, f32[1,250]{1,0:T(1,128)S(1)} %bitcast.10, f32[64,256,128]{2,1,0:T(8,128)S(1)} %bitcast.8), custom_call_target="tpu_custom_call" | custom-call | tf_op jit(solution)/shard_map/chemistry/pallas_call | solution.py:587
Async XLA Ops:
  0.6 56.2 %copy-start.1 = (f32[250]{0:T(256)S(1)}, f32[250]{0:T(256)}, u32[]{:S(2)}) copy-start(f32[250]{0:T(256)} %param.13) | copy-start | bytes 3004
  0.6 56.2 %copy-start = (f32[250,12]{0,1:T(8,128)S(1)}, f32[250,12]{0,1:T(8,128)}, u32[]{:S(2)}) copy-start(f32[250,12]{0,1:T(8,128)} %param.12) | copy-start | bytes 36004

commit v6 on v5

--- a/solution.py
+++ b/solution.py
@@ -145,10 +145,10 @@
         else:
             self.arrived(p, 8, 9, 12)
 
-        @pl.loop(0, 2)
+        @pl.loop(0, 1)
         def _(twice):
-            for inner in range(2):
-                pair = half * 4 + twice * 2 + inner
+            for inner in range(4):
+                pair = half * 4 + twice * 4 + inner
 
                 def level(fl):
                     start = pl.multiple_of(16 + fl * ITEMS, 16)
@@ -258,7 +258,7 @@
 
 
 SPECIES = 256
-UNROLL = 8
+UNROLL = 16
 HALO_COPIES = 75
 
 
@@ -524,7 +524,7 @@
     )(met_src, weights, dest, row, tracers)
 
 
-CHUNK = 16
+CHUNK = 32
 
 
 def thirds(value):

time: 64.3 us -> 63.4 us (0.986)
  Pallas kernels: 63.1 us -> 61.5 us
    pallas_call x1, Pallas kernels: 56.2 us -> 54.7 us  [transport_call(): pl.pallas_call(transport_kernel, out_shape=(pltpu.VMEM((1024, 128), F32),...]
where the time goes in v6:
time: 63.4 us; the launch traced here: 62.3 us
  Pallas kernels  61.5 us (97%)
  between operations  0.83 us (1%)
    pallas_call x1, Pallas kernels, transport_call(): pl.pallas_call(transport_kernel, out_shape=(pltpu.VMEM((1024, 128), F32),...  54.7 us
    pallas_call x1, Pallas kernels, chemistry_call(): pl.pallas_call(chemistry_kernel, out_shape=(jax.ShapeDtypeStruct((768, 12...  6.76 us

profile of v6, /device:TPU:0, one launch (start us, length us, event | category | flops | bytes accessed | tf_op | source)
XLA Modules:
  0.0 62.3 jit_solution(5457372772016605534)
XLA Ops:
  0.6 0.0 copy-start.1
  0.6 0.0 copy-start
  0.7 54.7 %transport.1 = (f32[1024,128]{1,0:T(8,128)S(1)}, f32[4,16,256,128]{3,2,1,0:T(8,128)S(1)}) custom-call(bf16[64,48,128]{2,1,0:T(8,128)(2,1)} %met_hbm.1, bf16[64,128,128]{2,1,0:T(8,128)(2,1)} %weight_hbm.1, s32[1,64]{1,0:T(1,128)} %bitcast.12, s32[1,64]{1,0:T(1,128)} %bitcast.13, f32[250,64,1,128]{3,2,1,0:T(1,128)} %bitcast.11), custom_call_target="tpu_custom_call" | custom-call | tf_op jit(solution)/shard_map/transport/pallas_call | solution.py:516
  55.4 0.0 copy-done.1
  55.4 0.0 copy-done
  55.4 6.8 %chemistry.1 = (f32[768,128]{1,0:T(8,128)}, f32[250,64,1,128]{3,2,1,0:T(1,128)}) custom-call(f32[1024,128]{1,0:T(8,128)S(1)} %get-tuple-element.6.mx_ref, f32[12,250]{1,0:T(8,128)S(1)} %bitcast.9, f32[1,250]{1,0:T(1,128)S(1)} %bitcast.10, f32[64,256,128]{2,1,0:T(8,128)S(1)} %bitcast.8), custom_call_target="tpu_custom_call" | custom-call | tf_op jit(solution)/shard_map/chemistry/pallas_call | solution.py:587
Async XLA Ops:
  0.6 54.8 %copy-start.1 = (f32[250]{0:T(256)S(1)}, f32[250]{0:T(256)}, u32[]{:S(2)}) copy-start(f32[250]{0:T(256)} %param.13) | copy-start | bytes 3004
  0.6 54.8 %copy-start = (f32[250,12]{0,1:T(8,128)S(1)}, f32[250,12]{0,1:T(8,128)}, u32[]{:S(2)}) copy-start(f32[250,12]{0,1:T(8,128)} %param.12) | copy-start | bytes 36004
